TPU v7x, 256 devices: a whole 4x4x8 slice. The times are simulated.
256 devices in a mesh: dp: 8 (over z), space: 32 (over x, y, core).
Axes of the slice: x: 4, y: 4, z: 8, core: 2. Of those that a mesh axis runs over, the one named last changes fastest.
Arguments:
- volume: bfloat16 [8, 32, 8, 16, 16, 256], P('dp', 'space'), may hold values from -6 to 6
- fine_filter: bfloat16 [3, 3, 3, 256, 256], P(None, None, None, 'dp'), may hold values from -0.078125 to 0.078125
- coarse_filter: bfloat16 [3, 3, 3, 256, 256], P(None, None, None, 'dp'), may hold values from -0.078125 to 0.078125
- fine_bias: float32 [256], replicated, may hold values from -3 to 3
- coarse_bias: float32 [256], replicated, may hold values from -3 to 3
Outputs:
- context: bfloat16 [8, 32, 8, 16, 16, 256], P('dp', 'space')
All inputs are finite; a program needn't handle non-finite values.
Results may differ from a plain program's by a relative error of at most 0.0047.
Values may be sent and summed in bfloat16 or wider, within the bound.
No kernel may reach another device: no remote copies, remote signals or barrier semaphores. Data moves between devices by JAX's collectives and lax.ppermute only.
A program may use at most 128 MiB of HBM per device.

v0:
```python
import jax
import jax.numpy as jnp
from jax import lax
from jax.sharding import PartitionSpec as P

X = 64
BX = 8


def filters(shard):
    return lax.all_gather(shard, "dp", axis=3, tiled=True)


def dense_taps(grid, weights, bias):
    items, length_x, length_y, length_z, channels = grid.shape
    padded = jnp.pad(grid, ((0, 0), (1, 1), (1, 1), (1, 1), (0, 0)))
    total = jnp.zeros(grid.shape, jnp.float32)
    for step_x in range(3):
        for step_y in range(3):
            window = padded[:, step_x : step_x + length_x, step_y : step_y + length_y]
            stacked = jnp.concatenate(
                [window[:, :, :, depth : depth + length_z] for depth in range(3)], axis=-1
            )
            total = total + jnp.dot(
                stacked,
                weights[step_x, step_y].reshape(3 * channels, channels),
                preferred_element_type=jnp.float32,
            )
    return (grid.astype(jnp.float32) + jax.nn.gelu(total + bias)).astype(jnp.bfloat16)


def fine_cosets(brick):
    size_x, size_y, size_z, channels = brick.shape
    split = brick.reshape(size_x // 4, 4, size_y // 4, 4, size_z // 4, 4, channels)
    return split.transpose(1, 3, 5, 0, 2, 4, 6).reshape(
        64, size_x // 4, size_y // 4, size_z // 4, channels
    )


def fine_bricks(cosets):
    count, along_u, along_v, along_w, channels = cosets.shape
    split = cosets.reshape(4, 4, 4, along_u, along_v, along_w, channels).transpose(
        3, 0, 4, 1, 5, 2, 6
    )
    return split.reshape(along_u * 4, along_v * 4, along_w * 4, channels)


def assemble(parts):
    items, devices, along_u, along_v, along_w, channels = parts.shape
    across_x = X // BX
    across_y = devices // across_x
    grid = parts.reshape(items, across_x, across_y, along_u, along_v, along_w, channels).transpose(
        0, 1, 3, 2, 4, 5, 6
    )
    return grid.reshape(items, across_x * along_u, across_y * along_v, along_w, channels)


def disassemble(grid, along_u, along_v):
    items, size_x, size_y, along_w, channels = grid.shape
    across_x = size_x // along_u
    across_y = size_y // along_v
    parts = grid.reshape(items, across_x, along_u, across_y, along_v, along_w, channels).transpose(
        0, 1, 3, 2, 4, 5, 6
    )
    return parts.reshape(1, items, across_x * across_y, along_u, along_v, along_w, channels)


def split_halves(grid):
    items, size_x, size_y, size_z, channels = grid.shape
    parts = grid.reshape(items, size_x // 2, 2, size_y // 2, 2, size_z // 2, 2, channels).transpose(
        0, 2, 4, 6, 1, 3, 5, 7
    )
    return parts.reshape(items * 8, size_x // 2, size_y // 2, size_z // 2, channels)


def join_halves(parts, items):
    count, half_x, half_y, half_z, channels = parts.shape
    grid = parts.reshape(items, 2, 2, 2, half_x, half_y, half_z, channels).transpose(
        0, 4, 1, 5, 2, 6, 3, 7
    )
    return grid.reshape(items, half_x * 2, half_y * 2, half_z * 2, channels)


def on_device(volume, fine_filter, coarse_filter, fine_bias, coarse_bias):
    brick = volume[0, 0]
    devices = lax.axis_size("space")
    fine_weights = filters(fine_filter)
    coarse_weights = filters(coarse_filter)
    cosets = fine_cosets(brick)
    outgoing = cosets.reshape((devices, 64 // devices, 1) + cosets.shape[1:])
    received = lax.all_to_all(outgoing, "space", split_axis=0, concat_axis=2, tiled=True)
    items = received.shape[1]
    along_u = received.shape[3]
    along_v = received.shape[4]
    grid = dense_taps(assemble(received[0]), fine_weights, fine_bias)
    finer = dense_taps(split_halves(grid), coarse_weights, coarse_bias)
    grid = join_halves(finer, items)
    returned = lax.all_to_all(
        disassemble(grid, along_u, along_v), "space", split_axis=2, concat_axis=0, tiled=True
    )
    brick = fine_bricks(returned.reshape(cosets.shape))
    return brick.reshape(volume.shape)


def solution(mesh):
    return jax.shard_map(
        on_device,
        mesh=mesh,
        in_specs=(
            P("dp", "space", None, None, None, None),
            P(None, None, None, "dp", None),
            P(None, None, None, "dp", None),
            P(),
            P(),
        ),
        out_specs=P("dp", "space", None, None, None, None),
        check_vma=False,
    )
```

profile of v0, /device:TPU:1, one launch (start us, length us, event | category | flops | bytes accessed | tf_op | source)
XLA Modules:
  0.0 164.3 jit_solution(2453152711800644022)
XLA Ops:
  6.5 0.7 all-gather.3.cloned.1.call-update
  7.3 1.3 reshape_squeeze.60
  8.6 1.6 copy.22
  10.2 8.6 %all-to-all-start = ((bf16[32,2,1,2,4,4,256]{6,5,4,3,1,2,0:T(4,128)(2,1)}), bf16[32,2,1,2,4,4,256]{6,5,4,3,1,2,0:T(4,128)(2,1)S(1)}, u32[]{:S(2)}, u32[]{:S(2)}) async-start(bf16[32,2,1,2,4,4,256]{6,5,4,3,1,2,0:T(4,128)(2,1)} %bitcast.2), calls=%async_computation | async-start | bytes 2097152 | tf_op jit(solution)/shard_map/all_to_all | solution.py:91
  18.8 0.7 all-gather.5.cloned.1.call-update
  19.5 16.2 %all-to-all-done = bf16[32,2,1,2,4,4,256]{6,5,4,3,1,2,0:T(4,128)(2,1)S(1)} async-done(((bf16[32,2,1,2,4,4,256]{6,5,4,3,1,2,0:T(4,128)(2,1)}), bf16[32,2,1,2,4,4,256]{6,5,4,3,1,2,0:T(4,128)(2,1)S(1)}, u32[]{:S(2)}, u32[]{:S(2)}) %all-to-all-start) | async-done | bytes 1048608 | tf_op jit(solution)/shard_map/all_to_all | solution.py:91
  35.7 0.5 copy.25
  36.5 3.2 %pad_slice_fusion.27 = (bf16[2,16,16,4,256]{4,2,3,1,0:T(8,128)(2,1)}, bf16[2,16,16,4,256]{4,2,3,1,0:T(8,128)(2,1)}, bf16[2,16,16,4,256]{4,2,3,1,0:T(8,128)(2,1)}...) fusion(bf16[2,16,16,4,256]{4,2,3,1,0:T(8,128)(2,1)S(1)} %reshape.19), kind=kLoop, calls=%fused_computation.27 | loop fusion | bytes 8388608 | tf_op jit(solution)/shard_map/slice | solution.py:22
  39.7 6.7 %pad_slice_fusion.28 = (bf16[2,16,16,4,256]{4,2,3,1,0:T(8,128)(2,1)S(1)}, bf16[2,16,16,4,256]{4,2,3,1,0:T(8,128)(2,1)}, bf16[2,16,16,4,256]{4,2,3,1,0:T(8,128)(2...) fusion(bf16[2,16,16,4,256]{4,2,3,1,0:T(8,128)(2,1)S(1)} %reshape.19), kind=kLoop, calls=%fused_computation.28 | loop fusion | bytes 20971520 | tf_op jit(solution)/shard_map/slice | solution.py:22
  46.5 14.9 %all-gather.3.cloned.1.call-done = bf16[3,3,3,256,256]{4,3,2,1,0:T(8,128)(2,1)} async-done(((bf16[3,3,3,32,256]{4,3,2,1,0:T(8,128)(2,1)}), bf16[3,3,3,256,256]{4,3,2,1,0:T(8,128)(2,1)}) %all-gather.3.cloned.1.call-update) | async-done | bytes 3538960 | tf_op jit(solution)/shard_map/all_gather | solution.py:11
  61.4 2.3 %fusion.149 = (bf16[1,1,3,256,256]{4,3,2,1,0:T(8,128)(2,1)S(1)}, bf16[1,1,3,256,256]{4,3,2,1,0:T(8,128)(2,1)S(1)}, bf16[1,1,3,256,256]{4,3,2,1,0:T(8,128)(2,1)S(...) fusion(bf16[3,3,3,256,256]{4,3,2,1,0:T(8,128)(2,1)} %all-gather, ...), kind=kLoop, calls=%fused_computation.199 | loop fusion | bytes 7077888 | tf_op jit(solution)/shard_map/slice | solution.py:26
  64.0 1.2 fusion.24
  65.2 0.3 copy-done.29
  65.5 0.3 copy-done.30
  65.9 1.2 fusion.6
  67.1 0.3 copy-done.26
  67.4 0.3 copy-done.27
  67.7 1.2 fusion.12
  68.9 0.3 copy-done.21
  69.2 0.3 copy-done.22
  69.6 1.2 fusion.18
  70.8 0.3 copy-done.15
  71.1 0.3 copy-done.16
  71.4 1.2 fusion.30
  72.6 0.3 copy-done.7
  73.0 0.3 copy-done.46
  73.3 1.2 fusion
  74.8 1.2 fusion.36
  76.0 0.3 copy-done.39
  76.4 0.3 copy-done.40
  76.7 1.2 fusion.42
  77.9 0.3 copy-done.1
  78.2 2.1 %fusion.116 = bf16[2,16,16,4,256]{4,2,3,1,0:T(8,128)(2,1)S(1)} fusion(f32[2,16,16,4,256]{4,2,3,1,0:T(8,128)S(1)} %fusion.42, f32[2,16,16,4,256]{4,2,3,1,0:T(8,128)S(1)} %fusion.36, f32[2,16,16,4,256]{4,2,3,1,0:T(8,128)S(1)} %fusion.30, f32[2,16,16,4,256]{4,2,3,1,0:T(8,128)S(1)} %fusion.24, f32[2,16,16,4,256]{4,2,3,1,0:T(8,128)S(1)} %fusion.18, ...), kind=kOutput, calls=%fused_computation.170 | convolution fusion | flops 825229312 | bytes 22414336 | tf_op jit(solution)/shard_map/dot_general | solution.py:24
  80.4 0.4 reshape.20
  81.0 2.8 %pad_slice_fusion.1 = (bf16[16,8,8,2,256]{4,2,3,1,0:T(8,128)(2,1)S(1)}, bf16[16,8,8,2,256]{4,2,3,1,0:T(8,128)(2,1)}, bf16[16,8,8,2,256]{4,2,3,1,0:T(8,128)(2,1)}...) fusion(bf16[16,8,8,2,256]{4,2,3,1,0:T(8,128)(2,1)S(1)} %bitcast.145), kind=kLoop, calls=%fused_computation.1 | loop fusion | bytes 8388608 | tf_op jit(solution)/shard_map/slice | solution.py:22
  83.8 6.5 %pad_slice_fusion.2 = (bf16[16,8,8,2,256]{4,2,3,1,0:T(8,128)(2,1)S(1)}, bf16[16,8,8,2,256]{4,2,3,1,0:T(8,128)(2,1)}, bf16[16,8,8,2,256]{4,2,3,1,0:T(8,128)(2,1)}...) fusion(bf16[16,8,8,2,256]{4,2,3,1,0:T(8,128)(2,1)S(1)} %bitcast.146), kind=kLoop, calls=%fused_computation.2 | loop fusion | bytes 20971520 | tf_op jit(solution)/shard_map/slice | solution.py:22
  90.3 20.1 %all-gather.5.cloned.1.call-done = bf16[3,3,3,256,256]{4,3,2,1,0:T(8,128)(2,1)} async-done(((bf16[3,3,3,32,256]{4,3,2,1,0:T(8,128)(2,1)}), bf16[3,3,3,256,256]{4,3,2,1,0:T(8,128)(2,1)}) %all-gather.5.cloned.1.call-update) | async-done | bytes 3538960 | tf_op jit(solution)/shard_map/all_gather | solution.py:11
  110.4 2.4 %fusion.148 = (bf16[1,1,3,256,256]{4,3,2,1,0:T(8,128)(2,1)S(1)}, bf16[1,1,3,256,256]{4,3,2,1,0:T(8,128)(2,1)S(1)}, bf16[1,1,3,256,256]{4,3,2,1,0:T(8,128)(2,1)S(...) fusion(bf16[3,3,3,256,256]{4,3,2,1,0:T(8,128)(2,1)} %all-gather, ...), kind=kLoop, calls=%fused_computation.198 | loop fusion | bytes 7077888 | tf_op jit(solution)/shard_map/slice | solution.py:26
  113.0 1.2 fusion.78
  114.3 0.3 copy-done.32
  114.6 0.3 copy-done.33
  114.9 1.2 fusion.60
  116.1 0.3 copy-done.24
  116.4 0.3 copy-done.47
  116.8 1.2 fusion.54
  118.0 0.3 copy-done.18
  118.3 0.3 copy-done.19
  118.6 1.2 fusion.66
  119.8 0.3 copy-done.12
  120.2 0.3 copy-done.13
  120.5 1.2 fusion.72
  121.7 0.3 copy-done.9
  122.0 0.3 copy-done.10
  122.3 1.2 fusion.84
  123.5 0.3 copy-done.5
  123.9 0.3 copy-done.45
  124.2 1.2 fusion.90
  126.0 1.2 fusion.96
  127.3 2.3 %fusion.125 = bf16[16,8,8,2,256]{4,2,3,1,0:T(8,128)(2,1)S(1)} fusion(f32[16,8,8,2,256]{4,2,3,1,0:T(8,128)S(1)} %fusion.96, f32[16,8,8,2,256]{4,2,3,1,0:T(8,128)S(1)} %fusion.90, f32[16,8,8,2,256]{4,2,3,1,0:T(8,128)S(1)} %fusion.84, f32[16,8,8,2,256]{4,2,3,1,0:T(8,128)S(1)} %fusion.78, f32[16,8,8,2,256]{4,2,3,1,0:T(8,128)S(1)} %fusion.72, ...), kind=kOutput, calls=%fused_computation.179 | convolution fusion | flops 825229312 | bytes 22414336 | tf_op jit(solution)/shard_map/dot_general | solution.py:24
  129.6 0.4 copy.27
  130.0 0.6 copy.50
  130.6 24.4 %all_to_all.30 = bf16[1,2,32,2,4,4,256]{6,5,4,3,1,0,2:T(4,128)(2,1)S(1)} all-to-all(bf16[1,2,32,2,4,4,256]{6,5,4,3,1,0,2:T(4,128)(2,1)S(1)} %bitcast.153), channel_id=1, replica_groups=mesh['dp'=8,'space'=32] {'space'}, dimensions={2} | all-to-all | bytes 2097152 | tf_op jit(solution)/shard_map/all_to_all | solution.py:98
  155.0 1.4 copy.30
  156.4 1.1 reshape_reshape.15
  (79 shorter events, 2.4 us)
Async XLA Ops:
  6.5 54.9 %all-gather.3.cloned.1.call-start = ((), (), s32[]{:S(2)}) async-start(), calls=%async_computation.2 | async-start | bytes 3981312 | tf_op jit(solution)/shard_map/all_gather | solution.py:11
  10.2 25.5 %all-to-all-start = ((bf16[32,2,1,2,4,4,256]{6,5,4,3,1,2,0:T(4,128)(2,1)}), bf16[32,2,1,2,4,4,256]{6,5,4,3,1,2,0:T(4,128)(2,1)S(1)}, u32[]{:S(2)}, u32[]{:S(2)}) async-start(bf16[32,2,1,2,4,4,256]{6,5,4,3,1,2,0:T(4,128)(2,1)} %bitcast.2), calls=%async_computation | async-start | bytes 2097152 | tf_op jit(solution)/shard_map/all_to_all | solution.py:91
  18.8 91.7 %all-gather.5.cloned.1.call-start = ((), (), s32[]{:S(2)}) async-start(), calls=%async_computation.3 | async-start | bytes 3981312 | tf_op jit(solution)/shard_map/all_gather | solution.py:11
  61.4 2.3 %copy-start.34 = (bf16[2,16,16,4,256]{4,2,3,1,0:T(8,128)(2,1)S(1)}, bf16[2,16,16,4,256]{4,2,3,1,0:T(8,128)(2,1)}, u32[]{:S(2)}) copy-start(bf16[2,16,16,4,256]{4,2,3,1,0:T(8,128)(2,1)} %get-tuple-element.61) | copy-start | bytes 3145732
  61.4 2.6 %copy-start.35 = (bf16[2,16,16,4,256]{4,2,3,1,0:T(8,128)(2,1)S(1)}, bf16[2,16,16,4,256]{4,2,3,1,0:T(8,128)(2,1)}, u32[]{:S(2)}) copy-start(bf16[2,16,16,4,256]{4,2,3,1,0:T(8,128)(2,1)} %get-tuple-element.62) | copy-start | bytes 3145732
  64.0 1.2 copy-start.28
  64.0 1.5 copy-start.29
  64.0 1.9 %copy-start.30 = (bf16[2,16,16,4,256]{4,2,3,1,0:T(8,128)(2,1)S(1)}, bf16[2,16,16,4,256]{4,2,3,1,0:T(8,128)(2,1)}, u32[]{:S(2)}) copy-start(bf16[2,16,16,4,256]{4,2,3,1,0:T(8,128)(2,1)} %get-tuple-element.54) | copy-start | bytes 3145732
  65.9 1.2 copy-start.25
  65.9 1.5 copy-start.26
  65.9 1.9 %copy-start.27 = (bf16[2,16,16,4,256]{4,2,3,1,0:T(8,128)(2,1)S(1)}, bf16[2,16,16,4,256]{4,2,3,1,0:T(8,128)(2,1)}, u32[]{:S(2)}) copy-start(bf16[2,16,16,4,256]{4,2,3,1,0:T(8,128)(2,1)} %get-tuple-element.57) | copy-start | bytes 3145732
  67.7 1.2 copy-start.20
  67.7 1.5 copy-start.21
  67.7 1.9 %copy-start.22 = (bf16[2,16,16,4,256]{4,2,3,1,0:T(8,128)(2,1)S(1)}, bf16[2,16,16,4,256]{4,2,3,1,0:T(8,128)(2,1)}, u32[]{:S(2)}) copy-start(bf16[2,16,16,4,256]{4,2,3,1,0:T(8,128)(2,1)} %get-tuple-element.60) | copy-start | bytes 3145732
  69.6 1.2 copy-start.14
  69.6 1.5 copy-start.15
  69.6 1.9 %copy-start.16 = (bf16[2,16,16,4,256]{4,2,3,1,0:T(8,128)(2,1)S(1)}, bf16[2,16,16,4,256]{4,2,3,1,0:T(8,128)(2,1)}, u32[]{:S(2)}) copy-start(bf16[2,16,16,4,256]{4,2,3,1,0:T(8,128)(2,1)} %get-tuple-element.65) | copy-start | bytes 3145732
  71.4 1.2 copy-start.6
  71.4 1.5 copy-start.7
  71.4 1.9 %copy-start.46 = (bf16[2,16,16,4,256]{4,2,3,1,0:T(8,128)(2,1)S(1)}, bf16[2,16,16,4,256]{4,2,3,1,0:T(8,128)(2,1)}, u32[]{:S(2)}) copy-start(bf16[2,16,16,4,256]{4,2,3,1,0:T(8,128)(2,1)} %get-tuple-element.74) | copy-start | bytes 3145732
  73.3 1.2 copy-start.3
  73.3 1.5 copy-start.44
  74.8 1.2 copy-start.38
  74.8 1.5 copy-start.39
  74.8 1.9 %copy-start.40 = (bf16[2,16,16,4,256]{4,2,3,1,0:T(8,128)(2,1)S(1)}, bf16[2,16,16,4,256]{4,2,3,1,0:T(8,128)(2,1)}, u32[]{:S(2)}) copy-start(bf16[2,16,16,4,256]{4,2,3,1,0:T(8,128)(2,1)} %get-tuple-element.72) | copy-start | bytes 3145732
  76.7 1.2 copy-start
  76.7 1.5 copy-start.1
  76.7 1.5 copy-start.48
  110.4 2.4 %copy-start.36 = (bf16[16,8,8,2,256]{4,2,3,1,0:T(8,128)(2,1)S(1)}, bf16[16,8,8,2,256]{4,2,3,1,0:T(8,128)(2,1)}, u32[]{:S(2)}) copy-start(bf16[16,8,8,2,256]{4,2,3,1,0:T(8,128)(2,1)} %get-tuple-element.35) | copy-start | bytes 3145732
  110.4 2.6 %copy-start.37 = (bf16[16,8,8,2,256]{4,2,3,1,0:T(8,128)(2,1)S(1)}, bf16[16,8,8,2,256]{4,2,3,1,0:T(8,128)(2,1)}, u32[]{:S(2)}) copy-start(bf16[16,8,8,2,256]{4,2,3,1,0:T(8,128)(2,1)} %get-tuple-element.36) | copy-start | bytes 3145732
  113.0 1.2 copy-start.31
  113.0 1.5 copy-start.32
  113.0 1.9 %copy-start.33 = (bf16[16,8,8,2,256]{4,2,3,1,0:T(8,128)(2,1)S(1)}, bf16[16,8,8,2,256]{4,2,3,1,0:T(8,128)(2,1)}, u32[]{:S(2)}) copy-start(bf16[16,8,8,2,256]{4,2,3,1,0:T(8,128)(2,1)} %get-tuple-element.28) | copy-start | bytes 3145732
  114.9 1.2 copy-start.23
  114.9 1.5 copy-start.24
  114.9 1.9 %copy-start.47 = (bf16[16,8,8,2,256]{4,2,3,1,0:T(8,128)(2,1)S(1)}, bf16[16,8,8,2,256]{4,2,3,1,0:T(8,128)(2,1)}, u32[]{:S(2)}) copy-start(bf16[16,8,8,2,256]{4,2,3,1,0:T(8,128)(2,1)} %get-tuple-element.48) | copy-start | bytes 3145732
  116.8 1.2 copy-start.17
  116.8 1.5 copy-start.18
  116.8 1.9 %copy-start.19 = (bf16[16,8,8,2,256]{4,2,3,1,0:T(8,128)(2,1)S(1)}, bf16[16,8,8,2,256]{4,2,3,1,0:T(8,128)(2,1)}, u32[]{:S(2)}) copy-start(bf16[16,8,8,2,256]{4,2,3,1,0:T(8,128)(2,1)} %get-tuple-element.31) | copy-start | bytes 3145732
  118.6 1.2 copy-start.11
  118.6 1.5 copy-start.12
  118.6 1.9 %copy-start.13 = (bf16[16,8,8,2,256]{4,2,3,1,0:T(8,128)(2,1)S(1)}, bf16[16,8,8,2,256]{4,2,3,1,0:T(8,128)(2,1)}, u32[]{:S(2)}) copy-start(bf16[16,8,8,2,256]{4,2,3,1,0:T(8,128)(2,1)} %get-tuple-element.34) | copy-start | bytes 3145732
  120.5 1.2 copy-start.8
  120.5 1.5 copy-start.9
  120.5 1.9 %copy-start.10 = (bf16[16,8,8,2,256]{4,2,3,1,0:T(8,128)(2,1)S(1)}, bf16[16,8,8,2,256]{4,2,3,1,0:T(8,128)(2,1)}, u32[]{:S(2)}) copy-start(bf16[16,8,8,2,256]{4,2,3,1,0:T(8,128)(2,1)} %get-tuple-element.39) | copy-start | bytes 3145732
  122.3 1.2 copy-start.4
  122.3 1.5 copy-start.5
  122.3 1.9 %copy-start.45 = (bf16[16,8,8,2,256]{4,2,3,1,0:T(8,128)(2,1)S(1)}, bf16[16,8,8,2,256]{4,2,3,1,0:T(8,128)(2,1)}, u32[]{:S(2)}) copy-start(bf16[16,8,8,2,256]{4,2,3,1,0:T(8,128)(2,1)} %get-tuple-element.43) | copy-start | bytes 3145732
  124.2 1.2 copy-start.41
  124.2 1.5 copy-start.42
  124.2 1.9 %copy-start.43 = (bf16[16,8,8,2,256]{4,2,3,1,0:T(8,128)(2,1)S(1)}, bf16[16,8,8,2,256]{4,2,3,1,0:T(8,128)(2,1)}, u32[]{:S(2)}) copy-start(bf16[16,8,8,2,256]{4,2,3,1,0:T(8,128)(2,1)} %get-tuple-element.46) | copy-start | bytes 3145732
  126.0 1.2 copy-start.2
  126.0 1.2 copy-start.49
Sparse Core Ops, SparseCore 0:
  9.1 52.2 all-gather.2
  63.2 47.2 all-gather.4
where the time goes:
time: 165 us; the launch traced here: 164 us
  waiting for transfers between devices  52.6 us (32%)
  local copies, waits for them, and re-layouts  41.6 us (25%)
  blocking collectives  24.4 us (15%)
  matrix products  23.4 us (14%)
  between operations  13.7 us (8%)
  starting transfers between devices  8.62 us (5%)
    all_gather x2, waiting for transfers between devices, filters(): return lax.all_gather(shard, 'dp', axis=3, tiled=True)  35 us
    all_to_all x1, blocking collectives, on_device(): lax.all_to_all(disassemble(grid, along_u, along_v), 'space', split_axis=2...  24.4 us
    dot_general x18, matrix products, dense_taps(): jnp.dot(stacked, weights[step_x, step_y].reshape(3 * channels, channels),...  23.4 us
    slice x4, local copies, waits for them, and re-layouts, dense_taps(): window[:, :, :, depth:depth + length_z]  19.3 us
    all_to_all x1, waiting for transfers between devices, on_device(): lax.all_to_all(outgoing, 'space', split_axis=0, concat_axis=2, tiled=True)  16.2 us
    unnamed x100, local copies, waits for them, and re-layouts  9.78 us
    all_to_all x1, starting transfers between devices, on_device(): lax.all_to_all(outgoing, 'space', split_axis=0, concat_axis=2, tiled=True)  8.58 us
    slice x2, local copies, waits for them, and re-layouts, dense_taps(): weights[step_x, step_y].reshape(3 * channels, channels)  4.72 us
  transfers between devices with their start and end apart: 3, of which 3 were waited for; matrix products, arithmetic and copies ran while one was open for 23% of the time, Pallas kernels for 0%

commit v1 on v0

v1 whole, which is shorter than its diff:
```python
import functools

import jax
import jax.numpy as jnp
from jax import lax
from jax.experimental import pallas as pl
from jax.experimental.pallas import tpu as pltpu
from jax.sharding import Mesh
from jax.sharding import PartitionSpec as P

C = 256
TAPS = 27
ROWS = TAPS * 32
HALF = ROWS // 2
COPIES = 16
PIECES = 18
VMEM = pl.BlockSpec(memory_space=pltpu.VMEM)
ANY = pl.BlockSpec(memory_space=pl.ANY)
SMEM = pl.BlockSpec(memory_space=pltpu.SMEM)


def one_hot(source):
    row = lax.broadcasted_iota(jnp.int32, (C, C), 0)
    column = lax.broadcasted_iota(jnp.int32, (C, C), 1)
    return jnp.where(column == source(row), 1.0, 0.0).astype(jnp.bfloat16)


def select(matrix, rows):
    return jnp.dot(matrix, rows, preferred_element_type=jnp.float32).astype(jnp.bfloat16)


def brick_row(r):
    py, pzh, pzl, zq, yq = r >> 6, (r >> 5) & 1, (r >> 4) & 1, (r >> 2) & 3, r & 3
    return (4 * yq + py) * 16 + 4 * zq + 2 * pzh + pzl


def brick_row_inverse(r):
    by, bz = r >> 4, r & 15
    return ((by & 3) << 6) + ((bz & 3) << 4) + ((bz >> 2) << 2) + (by >> 2)


def wire_row(r, shift):
    pzl, zq, xh, y = r >> 7, (r >> 5) & 3, (r >> 4) & 1, (r & 15) + shift
    found = ((y >> 2) << 6) + (xh << 5) + (pzl << 4) + (zq << 2) + (y & 3)
    return jnp.where((y >= 0) & (y < 16), found, -1)


def wire_row_inverse(r):
    j, xh, pzl, zq, yq = r >> 6, (r >> 5) & 1, (r >> 4) & 1, (r >> 2) & 3, r & 3
    return (pzl << 7) + (zq << 5) + (xh << 4) + (j << 2) + yq


def moved_row(r, shift):
    y = (r & 15) + shift
    return jnp.where((y >= 0) & (y < 16), r + shift, -1)


def all_of(copies):
    for copy in copies:
        copy.start()
    return copies


def stage_kernel(place, fine, coarse, message, held, sem):
    base = pl.multiple_of(place[1] * HALF, 16)
    parts = [pl.ds(n * HALF, HALF) for n in range(2)]
    loads = all_of(
        [
            pltpu.make_async_copy(rows.at[pl.ds(base, HALF)], held.at[part], sem.at[0, n])
            for n, (rows, part) in enumerate(zip((fine, coarse), parts))
        ]
    )
    stores = []
    for n, part in enumerate(parts):
        loads[n].wait()
        stores += all_of([pltpu.make_async_copy(held.at[part], message.at[part], sem.at[1, n])])
    for store in stores:
        store.wait()


def pack_kernel(brick, wire, held, packed, sem):
    loads = [pltpu.make_async_copy(brick.at[x], held.at[x], sem.at[0, x]) for x in range(8)]
    all_of([loads[x] for x in (0, 4, 1, 5, 2, 6, 3, 7)])
    order = one_hot(brick_row)
    stores = []
    for half in range(2):
        for x in (2 * half, 2 * half + 4, 2 * half + 1, 2 * half + 5):
            loads[x].wait()
        for px in (2 * half, 2 * half + 1):
            for xh in range(2):
                rows = select(order, held[px + 4 * xh])
                packed[px * 8 : px * 8 + 8, xh * 32 : xh * 32 + 32, :] = rows.reshape(8, 32, C)
        block = pl.ds(half * 16, 16)
        stores += all_of([pltpu.make_async_copy(packed.at[block], wire.at[block], sem.at[1, half])])
    for store in stores:
        store.wait()


def unpack_kernel(wire, brick, held, placed, sem):
    loads = all_of(
        [
            pltpu.make_async_copy(wire.at[pl.ds(px * 8, 8)], held.at[pl.ds(px * 8, 8)], sem.at[0, px])
            for px in range(4)
        ]
    )
    order = one_hot(brick_row_inverse)
    stores = []
    for half in range(2):
        loads[2 * half].wait()
        loads[2 * half + 1].wait()
        places = [(px, xh) for px in (2 * half, 2 * half + 1) for xh in range(2)]
        for px, xh in places:
            rows = held[px * 8 : px * 8 + 8, xh * 32 : xh * 32 + 32, :].reshape(C, C)
            placed[px + 4 * xh] = select(order, rows)
        for px, xh in places:
            x = px + 4 * xh
            stores += all_of([pltpu.make_async_copy(placed.at[x], brick.at[x], sem.at[1, x])])
    for store in stores:
        store.wait()


def weight_copies(place, own, moved, swapped, part, held, sem):
    k, core = place[0], place[1]
    copies = [(own, held.at[k])]
    for side, pieces in ((core, moved), (1 - core, swapped)):
        rows = pl.ds(pl.multiple_of(side * HALF, 16), HALF)
        for step in range(1, 4):
            for piece, owner in ((2 * step - 2, k - step + 8), (2 * step - 1, k + step)):
                source = pieces[piece].at[pl.ds(part * HALF, HALF)]
                copies.append((source, held.at[lax.rem(owner, 8), rows]))
        copies.append((pieces[6 + part], held.at[lax.rem(k + 4, 8), rows]))
    return [
        pltpu.make_async_copy(source, target, sem.at[n])
        for n, (source, target) in enumerate(copies)
    ]


def taps_of(shifted, held, step, tz_from_zi):
    left, right = [], []
    for tz, zi in tz_from_zi:
        for tx in range(3):
            for ty in range(3):
                slab = shifted[ty, :, zi, tx * step * 16 : tx * step * 16 + 256, :]
                left.append(slab.reshape(2 * 256, C))
                tap = (tx * 3 + ty) * 3 + tz
                right.append(held[:, tap * 32 : tap * 32 + 32, :].reshape(C, C))
    return jnp.dot(
        jnp.concatenate(left, axis=1),
        jnp.concatenate(right, axis=0),
        preferred_element_type=jnp.float32,
    )


def block_kernel(place, wire, fine_bias, coarse_bias, *rest):
    pieces = rest[:PIECES]
    out, received, near, far, fine, coarse, context, packed, sem = rest[PIECES:]
    loads = all_of(
        [
            pltpu.make_async_copy(
                wire.at[pl.ds(4 * i, 4)], received.at[pl.ds(4 * i, 4)], sem.at[0, i]
            )
            for i in range(8)
        ]
    )
    moved, swapped = pieces[2:10], pieces[10:]
    fine_copies = weight_copies(place, pieces[0], moved, swapped, 0, fine, sem.at[1])
    coarse_copies = weight_copies(place, pieces[1], moved, swapped, 1, coarse, sem.at[2])
    all_of(fine_copies)
    all_of(coarse_copies)
    zero = jnp.zeros((3, 2, 4, 32, C), jnp.bfloat16)
    near[:, :, :, 0:16, :] = zero[:, :, :, :16]
    near[:, :, :, 272:288, :] = zero[:, :, :, :16]
    far[:, :, :, 0:32, :] = zero
    far[:, :, :, 288:320, :] = zero
    for load in loads:
        load.wait()
    for ty in range(3):
        order = one_hot(functools.partial(wire_row, shift=ty - 1))
        for i in range(8):
            rows = select(order, received[4 * i : 4 * i + 4].reshape(C, C))
            near[ty, :, :, 16 + 32 * i : 48 + 32 * i, :] = rows.reshape(2, 4, 32, C)
    for copy in fine_copies:
        copy.wait()
    for zo in range(4):
        pairs = [(tz, zo + tz - 1) for tz in range(3) if 0 <= zo + tz - 1 < 4]
        total = taps_of(near, fine, 1, pairs)
        here = near[1, :, zo, 16:272, :].reshape(512, C).astype(jnp.float32)
        middle = (here + jax.nn.gelu(total + fine_bias[...])).astype(jnp.bfloat16)
        far[1, :, zo, 32:288, :] = middle.reshape(2, 256, C)
    for copy in coarse_copies:
        copy.wait()
    for ty in (0, 2):
        order = one_hot(functools.partial(moved_row, shift=2 * (ty - 1)))
        for pzl in range(2):
            for z in range(4):
                far[ty, pzl, z, 32:288, :] = select(order, far[1, pzl, z, 32:288, :])
    for zo in range(4):
        pairs = [(tz, zo + 2 * (tz - 1)) for tz in range(3) if 0 <= zo + 2 * (tz - 1) < 4]
        total = taps_of(far, coarse, 2, pairs)
        here = far[1, :, zo, 32:288, :].reshape(512, C).astype(jnp.float32)
        result = (here + jax.nn.gelu(total + coarse_bias[...])).astype(jnp.bfloat16)
        context[:, zo] = result.reshape(2, 256, C)
    order = one_hot(wire_row_inverse)
    for i in range(8):
        rows = select(order, context[:, :, 32 * i : 32 * i + 32, :].reshape(C, C))
        packed[4 * i : 4 * i + 4] = rows.reshape(4, 64, C)
    stores = all_of(
        [
            pltpu.make_async_copy(
                packed.at[pl.ds(4 * i, 4)], out.at[pl.ds(4 * i, 4)], sem.at[0, 8 + i]
            )
            for i in range(8)
        ]
    )
    for store in stores:
        store.wait()


def shift(value, by):
    return lax.ppermute(value, "dp", [(k, (k + by) % 8) for k in range(8)])


def swap(value):
    return lax.ppermute(value, "core", [(0, 1), (1, 0)])


def gather_filters(shards, place):
    own = [shard.reshape(ROWS, C) for shard in shards]
    message = pl.pallas_call(
        stage_kernel,
        out_shape=jax.ShapeDtypeStruct((ROWS, C), jnp.bfloat16),
        in_specs=[SMEM, ANY, ANY],
        out_specs=ANY,
        scratch_shapes=[pltpu.VMEM((ROWS, C), jnp.bfloat16), pltpu.SemaphoreType.DMA((2, 2))],
        name="stage",
    )(place, *own)
    forward = backward = message
    moved, swapped = [], []
    for step in range(1, 5):
        if step == 4:
            forward, backward = forward[:HALF], backward[HALF:]
        forward = shift(forward, 1)
        backward = shift(backward, -1)
        swapped.append(swap(forward))
        swapped.append(swap(backward))
        moved += [forward, backward]
    return (*own, *moved, *swapped)


def on_device(volume, fine_filter, coarse_filter, fine_bias, coarse_bias):
    brick = volume.reshape(8, 256, C)
    place = jnp.stack([lax.axis_index("dp"), lax.axis_index("core")]).astype(jnp.int32)
    wire_shape = jax.ShapeDtypeStruct((32, 64, C), jnp.bfloat16)

    pieces = gather_filters((fine_filter, coarse_filter), place)
    outgoing = pl.pallas_call(
        pack_kernel,
        out_shape=wire_shape,
        in_specs=[ANY],
        out_specs=ANY,
        scratch_shapes=[
            pltpu.VMEM((8, 256, C), jnp.bfloat16),
            pltpu.VMEM((32, 64, C), jnp.bfloat16),
            pltpu.SemaphoreType.DMA((2, 8)),
        ],
        name="pack",
    )(brick)
    received = lax.all_to_all(outgoing, ("x", "y", "core"), 0, 0, tiled=True)
    outgoing = pl.pallas_call(
        block_kernel,
        out_shape=wire_shape,
        in_specs=[SMEM, ANY, VMEM, VMEM] + [ANY] * PIECES,
        out_specs=ANY,
        scratch_shapes=[
            pltpu.VMEM((32, 64, C), jnp.bfloat16),
            pltpu.VMEM((3, 2, 4, 288, C), jnp.bfloat16),
            pltpu.VMEM((3, 2, 4, 320, C), jnp.bfloat16),
            pltpu.VMEM((8, ROWS, C), jnp.bfloat16),
            pltpu.VMEM((8, ROWS, C), jnp.bfloat16),
            pltpu.VMEM((2, 4, 256, C), jnp.bfloat16),
            pltpu.VMEM((32, 64, C), jnp.bfloat16),
            pltpu.SemaphoreType.DMA((3, COPIES)),
        ],
        name="block",
    )(place, received, fine_bias.reshape(1, C), coarse_bias.reshape(1, C), *pieces)
    received = lax.all_to_all(outgoing, ("x", "y", "core"), 0, 0, tiled=True)
    brick = pl.pallas_call(
        unpack_kernel,
        out_shape=jax.ShapeDtypeStruct((8, 256, C), jnp.bfloat16),
        in_specs=[ANY],
        out_specs=ANY,
        scratch_shapes=[
            pltpu.VMEM((32, 64, C), jnp.bfloat16),
            pltpu.VMEM((8, 256, C), jnp.bfloat16),
            pltpu.SemaphoreType.DMA((2, 8)),
        ],
        name="unpack",
    )(received)
    return brick.reshape(volume.shape)


def solution(mesh):
    grid = Mesh(mesh.devices.reshape(8, 4, 4, 2), ("dp", "x", "y", "core"))
    space = ("x", "y", "core")
    return jax.shard_map(
        on_device,
        mesh=grid,
        in_specs=(
            P("dp", space, None, None, None, None),
            P(None, None, None, "dp", None),
            P(None, None, None, "dp", None),
            P(),
            P(),
        ),
        out_specs=P("dp", space, None, None, None, None),
        check_vma=False,
    )
```

time: 165 us -> 104 us (0.63)
  local copies, waits for them, and re-layouts: 41.6 us -> 0.08 us
  waiting for transfers between devices: 52.6 us -> 25.1 us
  Pallas kernels: 0 us -> 25.1 us
  matrix products: 23.4 us -> 0 us
  starting transfers between devices: 8.62 us -> 28 us
  between operations: 13.7 us -> 0.39 us
    all_gather x2 -> x0, waiting for transfers between devices: 35 us -> none  [filters(): return lax.all_gather(shard, 'dp', axis=3, tiled=True)]
    ppermute x0 -> x16, waiting for transfers between devices: none -> 25.1 us  [the longest x8 23.6 us: shift(): return lax.ppermute(value, 'dp', [(k, (k + by) % 8) for k in range(8)])]
    pallas_call x0 -> x4, Pallas kernels: none -> 25.1 us  [the longest x1 17.5 us: on_device(): pl.pallas_call(block_kernel, out_shape=wire_shape, in_specs=[SMEM, ANY, V...]
    slice x6 -> x2, local copies, waits for them, and re-layouts: 24 us -> 0.03 us  [gather_filters(): forward, backward = (forward[:HALF], backward[HALF:])]
    dot_general x18 -> x0, matrix products: 23.4 us -> none  [dense_taps(): jnp.dot(stacked, weights[step_x, step_y].reshape(3 * channels, channels),...]
    ppermute x0 -> x16, starting transfers between devices: none -> 19.1 us  [the longest x8 14.6 us: shift(): return lax.ppermute(value, 'dp', [(k, (k + by) % 8) for k in range(8)])]
    all_to_all x1, waiting for transfers between devices: 16.2 us -> 0.01 us  [on_device(): received = lax.all_to_all(outgoing, ('x', 'y', 'core'), 0, 0, tiled=True)]
    unnamed x100 -> x24, local copies, waits for them, and re-layouts: 9.78 us -> 0.05 us
  transfers between devices with their start and end apart: 3 -> 17, of which waited for: 3 -> 5; matrix products, arithmetic and copies ran while one was open for 23% -> 0% of each run, Pallas kernels for 0% -> 3%
where the time goes in v1:
time: 104 us
  starting transfers between devices  28 us (27%)
  Pallas kernels  25.1 us (24%)
  waiting for transfers between devices  25.1 us (24%)
  blocking collectives  24.3 us (23%)
    all_to_all x1, blocking collectives, on_device(): received = lax.all_to_all(outgoing, ('x', 'y', 'core'), 0, 0, tiled=True)  24.3 us
    ppermute x8, waiting for transfers between devices, shift(): return lax.ppermute(value, 'dp', [(k, (k + by) % 8) for k in range(8)])  23.6 us
    pallas_call x1, Pallas kernels, on_device(): pl.pallas_call(block_kernel, out_shape=wire_shape, in_specs=[SMEM, ANY, V...  17.5 us
    ppermute x8, starting transfers between devices, shift(): return lax.ppermute(value, 'dp', [(k, (k + by) % 8) for k in range(8)])  14.6 us
    all_to_all x1, starting transfers between devices, on_device(): received = lax.all_to_all(outgoing, ('x', 'y', 'core'), 0, 0, tiled=True)  8.9 us
    ppermute x8, starting transfers between devices, swap(): return lax.ppermute(value, 'core', [(0, 1), (1, 0)])  4.44 us
    pallas_call x1, Pallas kernels, on_device(): pl.pallas_call(pack_kernel, out_shape=wire_shape, in_specs=[ANY], out_spe...  2.64 us
    pallas_call x1, Pallas kernels, on_device(): pl.pallas_call(unpack_kernel, out_shape=jax.ShapeDtypeStruct((8, 256, C),...  2.56 us
  transfers between devices with their start and end apart: 17, of which 5 were waited for; matrix products, arithmetic and copies ran while one was open for 0% of the time, Pallas kernels for 3%

profile of v1, /device:TPU:1, one launch (start us, length us, event | category | flops | bytes accessed | tf_op | source)
XLA Modules:
  0.0 103.5 jit_solution(17299053508774088458)
XLA Ops:
  0.0 0.6 pad_add_fusion.place
  0.6 2.4 %stage.1 = bf16[864,256]{1,0:T(8,128)(2,1)} custom-call(s32[2]{0:T(128)} %pad_add_fusion.place, bf16[864,256]{1,0:T(8,128)(2,1)} %bitcast.8, bf16[864,256]{1,0:T(8,128)(2,1)} %bitcast.10), custom_call_target="tpu_custom_call" | custom-call | tf_op jit(solution)/shard_map/stage/pallas_call | solution.py:229
  3.0 2.5 %collective-permute-start = (bf16[864,256]{1,0:T(8,128)(2,1)}, bf16[864,256]{1,0:T(8,128)(2,1)S(1)}, u32[]{:S(2)}, u32[]{:S(2)}) collective-permute-start(bf16[864,256]{1,0:T(8,128)(2,1)} %stage.1), channel_id=1, source_target_pairs={{0,32},{32,64},{64,96},{96,128},{128,160},{160,192},{192,224},{224... | collective-permute-start | bytes 1327112 | tf_op jit(solution)/shard_map/ppermute | solution.py:220
  5.6 4.0 %collective-permute-start.1 = (bf16[864,256]{1,0:T(8,128)(2,1)}, bf16[864,256]{1,0:T(8,128)(2,1)S(1)}, u32[]{:S(2)}, u32[]{:S(2)}) collective-permute-start(bf16[864,256]{1,0:T(8,128)(2,1)} %stage.1), channel_id=1, source_target_pairs={{0,224},{32,0},{64,32},{96,64},{128,96},{160,128},{192,160},{224,1... | collective-permute-start | bytes 1327112 | tf_op jit(solution)/shard_map/ppermute | solution.py:220
  9.6 10.0 %collective-permute-done.rest_2_ = bf16[864,256]{1,0:T(8,128)(2,1)S(1)} collective-permute-done((bf16[864,256]{1,0:T(8,128)(2,1)}, bf16[864,256]{1,0:T(8,128)(2,1)S(1)}, u32[]{:S(2)}, u32[]{:S(2)}) %collective-permute-start) | collective-permute-done | bytes 442400 | tf_op jit(solution)/shard_map/ppermute | solution.py:220
  19.6 0.0 copy-start.3
  19.6 0.0 collective-permute-start.2
  19.6 0.0 collective-permute-done.1.rest_3_
  19.6 0.0 copy-start.4
  19.6 2.7 %collective-permute-start.3 = (bf16[864,256]{1,0:T(8,128)(2,1)S(1)}, bf16[864,256]{1,0:T(8,128)(2,1)}, u32[]{:S(2)}, u32[]{:S(2)}) collective-permute-start(bf16[864,256]{1,0:T(8,128)(2,1)S(1)} %collective-permute-done.1.rest_3_), channel_id=1, source_target_pairs={{0,224},{32,0},{64,32},{96,64},{128,96},{160,128},{192,160},{224,1... | collective-permute-start | bytes 1327112 | tf_op jit(solution)/shard_map/ppermute | solution.py:220
  22.3 2.6 %pack.1 = bf16[32,64,256]{2,1,0:T(8,128)(2,1)} custom-call(bf16[8,256,256]{2,1,0:T(8,128)(2,1)} %bitcast.12), custom_call_target="tpu_custom_call" | custom-call | tf_op jit(solution)/shard_map/pack/pallas_call | solution.py:256
  24.9 8.9 %all-to-all-start = ((bf16[32,64,256]{2,1,0:T(8,128)(2,1)}), bf16[32,64,256]{2,1,0:T(8,128)(2,1)S(1)}, u32[]{:S(2)}, u32[]{:S(2)}) async-start(bf16[32,64,256]{2,1,0:T(8,128)(2,1)} %pack.1), calls=%async_computation | async-start | bytes 2097152 | tf_op jit(solution)/shard_map/all_to_all | solution.py:268
  33.8 0.0 collective-permute-done.2.rest_4_
  33.9 0.0 copy-start.5
  33.9 0.1 collective-permute-start.4
  34.0 0.0 collective-permute-done.3.rest_5_
  34.0 2.7 %collective-permute-start.5 = (bf16[864,256]{1,0:T(8,128)(2,1)}, bf16[864,256]{1,0:T(8,128)(2,1)S(1)}, u32[]{:S(2)}, u32[]{:S(2)}) collective-permute-start(bf16[864,256]{1,0:T(8,128)(2,1)} %collective-permute-done.3.rest_5_), channel_id=1, source_target_pairs={{0,224},{32,0},{64,32},{96,64},{128,96},{160,128},{192,160},{224,1... | collective-permute-start | bytes 1327112 | tf_op jit(solution)/shard_map/ppermute | solution.py:220
  36.6 0.0 copy-done.3
  36.6 0.8 collective-permute-start.8
  37.4 0.0 copy-done.4
  37.4 0.1 collective-permute-start.9
  37.5 0.4 collective-permute-start.10
  37.9 8.7 %collective-permute-done.4.rest_6_ = bf16[864,256]{1,0:T(8,128)(2,1)S(1)} collective-permute-done((bf16[864,256]{1,0:T(8,128)(2,1)S(1)}, bf16[864,256]{1,0:T(8,128)(2,1)S(1)}, u32[]{:S(2)}, u32[]{:S(2)}) %collective-permute-start.4) | collective-permute-done | bytes 442400 | tf_op jit(solution)/shard_map/ppermute | solution.py:220
  46.6 0.0 copy-start.1
  46.6 1.1 %collective-permute-start.11 = (bf16[864,256]{1,0:T(8,128)(2,1)}, bf16[864,256]{1,0:T(8,128)(2,1)}, u32[]{:S(2)}, u32[]{:S(2)}) collective-permute-start(bf16[864,256]{1,0:T(8,128)(2,1)} %collective-permute-done.3.rest_5_), channel_id=1, source_target_pairs={{0,1},{1,0},{2,3},{3,2},{4,5},{5,4},{6,7},{7,6},{8,9},{9,8},{10,11... | collective-permute-start | bytes 1327112 | tf_op jit(solution)/shard_map/ppermute | solution.py:224
  47.8 0.0 collective-permute-done.5.rest_7_
  47.8 0.0 copy-start.2
  47.8 0.1 collective-permute-start.6
  47.9 0.0 collective-permute-done.8.rest_10_
  47.9 0.0 copy-done.1
  47.9 0.0 copy-start.6
  47.9 0.6 collective-permute-start.12
  48.5 0.0 collective-permute-done.9.rest_11_
  48.5 0.0 copy-start.7
  48.5 0.1 collective-permute-start.13
  48.6 0.0 collective-permute-done.10.rest_12_
  48.6 0.0 copy-start.8
  48.6 2.6 %collective-permute-start.7 = (bf16[432,256]{1,0:T(8,128)(2,1)S(1)}, bf16[432,256]{1,0:T(8,128)(2,1)}, u32[]{:S(2)}, u32[]{:S(2)}) collective-permute-start(bf16[432,256]{1,0:T(8,128)(2,1)S(1)} %slice.9), channel_id=1, source_target_pairs={{0,224},{32,0},{64,32},{96,64},{128,96},{160,128},{192,160},{224,1... | collective-permute-start | bytes 663560 | tf_op jit(solution)/shard_map/ppermute | solution.py:220
  51.2 4.9 %collective-permute-done.6.rest_8_ = bf16[432,256]{1,0:T(8,128)(2,1)S(1)} collective-permute-done((bf16[432,256]{1,0:T(8,128)(2,1)S(1)}, bf16[432,256]{1,0:T(8,128)(2,1)S(1)}, u32[]{:S(2)}, u32[]{:S(2)}) %collective-permute-start.6) | collective-permute-done | bytes 221216 | tf_op jit(solution)/shard_map/ppermute | solution.py:220
  56.0 0.0 copy-start.11
  56.1 0.9 collective-permute-start.14
  56.9 0.0 collective-permute-done.7.rest_9_
  56.9 0.0 copy-done.6
  56.9 0.0 copy-done.7
  56.9 0.0 copy-done.8
  56.9 0.5 collective-permute-start.15
  57.4 0.0 all-to-all-done.wire
  57.4 0.0 copy-start
  57.5 0.0 collective-permute-done.11.rest_13_
  57.5 0.0 collective-permute-done.12.rest_14_
  57.5 0.0 copy-start.9
  57.5 0.0 collective-permute-done.13.rest_15_
  57.5 0.0 copy-start.10
  57.5 0.7 collective-permute-done.14.rest_16_
  58.1 0.9 collective-permute-done.15.rest_17_
  59.0 0.0 copy-done.5
  59.0 0.0 copy-done.2
  59.0 0.0 copy-done.11
  59.0 0.0 copy-done
  59.0 0.0 copy-done.9
  59.1 0.0 copy-done.10
  59.1 17.5 %block.1 = bf16[32,64,256]{2,1,0:T(8,128)(2,1)} custom-call(s32[2]{0:T(128)} %pad_add_fusion.place, bf16[32,64,256]{2,1,0:T(8,128)(2,1)} %copy-done, f32[1,256]{1,0:T(1,128)} %bitcast.13, f32[1,256]{1,0:T(1,128)} %bitcast.14, bf16[864,256]{1,0:T(8,128)(2,1)} %bitcast.9, bf16[864,256]{1,0:T(8,128)(2,1)} %bitcast.11, bf16[864,256]{1,0:T(8,128)(2,1)} %copy-done.3, ...), custom_call_target="tpu_custom_call" | custom-call | tf_op jit(solution)/shard_map/block/pallas_call | solution.py:269
  76.5 24.3 %all_to_all.10.wire = bf16[32,64,256]{2,1,0:T(8,128)(2,1)} all-to-all(bf16[32,64,256]{2,1,0:T(8,128)(2,1)} %block.1), channel_id=1, replica_groups=mesh['dp'=8,'x'=4,'y'=4,'core'=2] {'x','y','core'}, dimensions={0} | all-to-all | bytes 2097152 | tf_op jit(solution)/shard_map/all_to_all | solution.py:286
  100.8 2.6 %unpack.1 = bf16[8,256,256]{2,1,0:T(8,128)(2,1)} custom-call(bf16[32,64,256]{2,1,0:T(8,128)(2,1)} %all_to_all.10.wire), custom_call_target="tpu_custom_call" | custom-call | tf_op jit(solution)/shard_map/unpack/pallas_call | solution.py:287
  (2 shorter events, 0.0 us)
Async XLA Ops:
  3.0 16.6 %collective-permute-start = (bf16[864,256]{1,0:T(8,128)(2,1)}, bf16[864,256]{1,0:T(8,128)(2,1)S(1)}, u32[]{:S(2)}, u32[]{:S(2)}) collective-permute-start(bf16[864,256]{1,0:T(8,128)(2,1)} %stage.1), channel_id=1, source_target_pairs={{0,32},{32,64},{64,96},{96,128},{128,160},{160,192},{192,224},{224... | collective-permute-start | bytes 1327112 | tf_op jit(solution)/shard_map/ppermute | solution.py:220
  5.6 14.0 %collective-permute-start.1 = (bf16[864,256]{1,0:T(8,128)(2,1)}, bf16[864,256]{1,0:T(8,128)(2,1)S(1)}, u32[]{:S(2)}, u32[]{:S(2)}) collective-permute-start(bf16[864,256]{1,0:T(8,128)(2,1)} %stage.1), channel_id=1, source_target_pairs={{0,224},{32,0},{64,32},{96,64},{128,96},{160,128},{192,160},{224,1... | collective-permute-start | bytes 1327112 | tf_op jit(solution)/shard_map/ppermute | solution.py:220
  19.6 17.0 %copy-start.3 = (bf16[864,256]{1,0:T(8,128)(2,1)}, bf16[864,256]{1,0:T(8,128)(2,1)S(1)}, u32[]{:S(2)}) copy-start(bf16[864,256]{1,0:T(8,128)(2,1)S(1)} %collective-permute-done.rest_2_) | copy-start | bytes 1327108
  19.6 14.2 %collective-permute-start.2 = (bf16[864,256]{1,0:T(8,128)(2,1)S(1)}, bf16[864,256]{1,0:T(8,128)(2,1)S(1)}, u32[]{:S(2)}, u32[]{:S(2)}) collective-permute-start(bf16[864,256]{1,0:T(8,128)(2,1)S(1)} %collective-permute-done.rest_2_), channel_id=1, source_target_pairs={{0,32},{32,64},{64,96},{96,128},{128,160},{160,192},{192,224},{224... | collective-permute-start | bytes 1327112 | tf_op jit(solution)/shard_map/ppermute | solution.py:220
  19.6 17.8 %copy-start.4 = (bf16[864,256]{1,0:T(8,128)(2,1)}, bf16[864,256]{1,0:T(8,128)(2,1)S(1)}, u32[]{:S(2)}) copy-start(bf16[864,256]{1,0:T(8,128)(2,1)S(1)} %collective-permute-done.1.rest_3_) | copy-start | bytes 1327108
  19.6 14.3 %collective-permute-start.3 = (bf16[864,256]{1,0:T(8,128)(2,1)S(1)}, bf16[864,256]{1,0:T(8,128)(2,1)}, u32[]{:S(2)}, u32[]{:S(2)}) collective-permute-start(bf16[864,256]{1,0:T(8,128)(2,1)S(1)} %collective-permute-done.1.rest_3_), channel_id=1, source_target_pairs={{0,224},{32,0},{64,32},{96,64},{128,96},{160,128},{192,160},{224,1... | collective-permute-start | bytes 1327112 | tf_op jit(solution)/shard_map/ppermute | solution.py:220
  24.9 32.5 %all-to-all-start = ((bf16[32,64,256]{2,1,0:T(8,128)(2,1)}), bf16[32,64,256]{2,1,0:T(8,128)(2,1)S(1)}, u32[]{:S(2)}, u32[]{:S(2)}) async-start(bf16[32,64,256]{2,1,0:T(8,128)(2,1)} %pack.1), calls=%async_computation | async-start | bytes 2097152 | tf_op jit(solution)/shard_map/all_to_all | solution.py:268
  33.9 25.2 %copy-start.5 = (bf16[864,256]{1,0:T(8,128)(2,1)}, bf16[864,256]{1,0:T(8,128)(2,1)S(1)}, u32[]{:S(2)}) copy-start(bf16[864,256]{1,0:T(8,128)(2,1)S(1)} %collective-permute-done.2.rest_4_) | copy-start | bytes 1327108
  33.9 12.8 %collective-permute-start.4 = (bf16[864,256]{1,0:T(8,128)(2,1)S(1)}, bf16[864,256]{1,0:T(8,128)(2,1)S(1)}, u32[]{:S(2)}, u32[]{:S(2)}) collective-permute-start(bf16[864,256]{1,0:T(8,128)(2,1)S(1)} %collective-permute-done.2.rest_4_), channel_id=1, source_target_pairs={{0,32},{32,64},{64,96},{96,128},{128,160},{160,192},{192,224},{224... | collective-permute-start | bytes 1327112 | tf_op jit(solution)/shard_map/ppermute | solution.py:220
  34.0 13.8 %collective-permute-start.5 = (bf16[864,256]{1,0:T(8,128)(2,1)}, bf16[864,256]{1,0:T(8,128)(2,1)S(1)}, u32[]{:S(2)}, u32[]{:S(2)}) collective-permute-start(bf16[864,256]{1,0:T(8,128)(2,1)} %collective-permute-done.3.rest_5_), channel_id=1, source_target_pairs={{0,224},{32,0},{64,32},{96,64},{128,96},{160,128},{192,160},{224,1... | collective-permute-start | bytes 1327112 | tf_op jit(solution)/shard_map/ppermute | solution.py:220
  36.6 11.3 %collective-permute-start.8 = (bf16[864,256]{1,0:T(8,128)(2,1)S(1)}, bf16[864,256]{1,0:T(8,128)(2,1)S(1)}, u32[]{:S(2)}, u32[]{:S(2)}) collective-permute-start(bf16[864,256]{1,0:T(8,128)(2,1)S(1)} %collective-permute-done.rest_2_), channel_id=1, source_target_pairs={{0,1},{1,0},{2,3},{3,2},{4,5},{5,4},{6,7},{7,6},{8,9},{9,8},{10,11... | collective-permute-start | bytes 1327112 | tf_op jit(solution)/shard_map/ppermute | solution.py:224
  37.4 11.1 %collective-permute-start.9 = (bf16[864,256]{1,0:T(8,128)(2,1)S(1)}, bf16[864,256]{1,0:T(8,128)(2,1)S(1)}, u32[]{:S(2)}, u32[]{:S(2)}) collective-permute-start(bf16[864,256]{1,0:T(8,128)(2,1)S(1)} %collective-permute-done.1.rest_3_), channel_id=1, source_target_pairs={{0,1},{1,0},{2,3},{3,2},{4,5},{5,4},{6,7},{7,6},{8,9},{9,8},{10,11... | collective-permute-start | bytes 1327112 | tf_op jit(solution)/shard_map/ppermute | solution.py:224
  37.5 11.1 %collective-permute-start.10 = (bf16[864,256]{1,0:T(8,128)(2,1)S(1)}, bf16[864,256]{1,0:T(8,128)(2,1)S(1)}, u32[]{:S(2)}, u32[]{:S(2)}) collective-permute-start(bf16[864,256]{1,0:T(8,128)(2,1)S(1)} %collective-permute-done.2.rest_4_), channel_id=1, source_target_pairs={{0,1},{1,0},{2,3},{3,2},{4,5},{5,4},{6,7},{7,6},{8,9},{9,8},{10,11... | collective-permute-start | bytes 1327112 | tf_op jit(solution)/shard_map/ppermute | solution.py:224
  46.6 1.3 %copy-start.1 = (bf16[864,256]{1,0:T(8,128)(2,1)}, bf16[864,256]{1,0:T(8,128)(2,1)S(1)}, u32[]{:S(2)}) copy-start(bf16[864,256]{1,0:T(8,128)(2,1)S(1)} %collective-permute-done.4.rest_6_) | copy-start | bytes 1327108
  46.6 10.8 %collective-permute-start.11 = (bf16[864,256]{1,0:T(8,128)(2,1)}, bf16[864,256]{1,0:T(8,128)(2,1)}, u32[]{:S(2)}, u32[]{:S(2)}) collective-permute-start(bf16[864,256]{1,0:T(8,128)(2,1)} %collective-permute-done.3.rest_5_), channel_id=1, source_target_pairs={{0,1},{1,0},{2,3},{3,2},{4,5},{5,4},{6,7},{7,6},{8,9},{9,8},{10,11... | collective-permute-start | bytes 1327112 | tf_op jit(solution)/shard_map/ppermute | solution.py:224
  47.8 11.3 %copy-start.2 = (bf16[864,256]{1,0:T(8,128)(2,1)}, bf16[864,256]{1,0:T(8,128)(2,1)S(1)}, u32[]{:S(2)}) copy-start(bf16[864,256]{1,0:T(8,128)(2,1)S(1)} %collective-permute-done.5.rest_7_) | copy-start | bytes 1327108
  47.8 8.3 %collective-permute-start.6 = (bf16[432,256]{1,0:T(8,128)(2,1)S(1)}, bf16[432,256]{1,0:T(8,128)(2,1)S(1)}, u32[]{:S(2)}, u32[]{:S(2)}) collective-permute-start(bf16[432,256]{1,0:T(8,128)(2,1)S(1)} %slice.8), channel_id=1, source_target_pairs={{0,32},{32,64},{64,96},{96,128},{128,160},{160,192},{192,224},{224... | collective-permute-start | bytes 663560 | tf_op jit(solution)/shard_map/ppermute | solution.py:220
  47.9 9.0 %copy-start.6 = (bf16[864,256]{1,0:T(8,128)(2,1)}, bf16[864,256]{1,0:T(8,128)(2,1)S(1)}, u32[]{:S(2)}) copy-start(bf16[864,256]{1,0:T(8,128)(2,1)S(1)} %collective-permute-done.8.rest_10_) | copy-start | bytes 1327108
  47.9 9.5 %collective-permute-start.12 = (bf16[864,256]{1,0:T(8,128)(2,1)S(1)}, bf16[864,256]{1,0:T(8,128)(2,1)S(1)}, u32[]{:S(2)}, u32[]{:S(2)}) collective-permute-start(bf16[864,256]{1,0:T(8,128)(2,1)S(1)} %collective-permute-done.4.rest_6_), channel_id=1, source_target_pairs={{0,1},{1,0},{2,3},{3,2},{4,5},{5,4},{6,7},{7,6},{8,9},{9,8},{10,11... | collective-permute-start | bytes 1327112 | tf_op jit(solution)/shard_map/ppermute | solution.py:224
  48.5 8.4 %copy-start.7 = (bf16[864,256]{1,0:T(8,128)(2,1)}, bf16[864,256]{1,0:T(8,128)(2,1)S(1)}, u32[]{:S(2)}) copy-start(bf16[864,256]{1,0:T(8,128)(2,1)S(1)} %collective-permute-done.9.rest_11_) | copy-start | bytes 1327108
  48.5 9.0 %collective-permute-start.13 = (bf16[864,256]{1,0:T(8,128)(2,1)S(1)}, bf16[864,256]{1,0:T(8,128)(2,1)S(1)}, u32[]{:S(2)}, u32[]{:S(2)}) collective-permute-start(bf16[864,256]{1,0:T(8,128)(2,1)S(1)} %collective-permute-done.5.rest_7_), channel_id=1, source_target_pairs={{0,1},{1,0},{2,3},{3,2},{4,5},{5,4},{6,7},{7,6},{8,9},{9,8},{10,11... | collective-permute-start | bytes 1327112 | tf_op jit(solution)/shard_map/ppermute | solution.py:224
  48.6 8.3 %copy-start.8 = (bf16[864,256]{1,0:T(8,128)(2,1)}, bf16[864,256]{1,0:T(8,128)(2,1)S(1)}, u32[]{:S(2)}) copy-start(bf16[864,256]{1,0:T(8,128)(2,1)S(1)} %collective-permute-done.10.rest_12_) | copy-start | bytes 1327108
  48.6 8.3 %collective-permute-start.7 = (bf16[432,256]{1,0:T(8,128)(2,1)S(1)}, bf16[432,256]{1,0:T(8,128)(2,1)}, u32[]{:S(2)}, u32[]{:S(2)}) collective-permute-start(bf16[432,256]{1,0:T(8,128)(2,1)S(1)} %slice.9), channel_id=1, source_target_pairs={{0,224},{32,0},{64,32},{96,64},{128,96},{160,128},{192,160},{224,1... | collective-permute-start | bytes 663560 | tf_op jit(solution)/shard_map/ppermute | solution.py:220
  56.0 3.0 %copy-start.11 = (bf16[432,256]{1,0:T(8,128)(2,1)}, bf16[432,256]{1,0:T(8,128)(2,1)S(1)}, u32[]{:S(2)}) copy-start(bf16[432,256]{1,0:T(8,128)(2,1)S(1)} %collective-permute-done.6.rest_8_) | copy-start | bytes 663556
  56.1 2.1 %collective-permute-start.14 = (bf16[432,256]{1,0:T(8,128)(2,1)S(1)}, bf16[432,256]{1,0:T(8,128)(2,1)}, u32[]{:S(2)}, u32[]{:S(2)}) collective-permute-start(bf16[432,256]{1,0:T(8,128)(2,1)S(1)} %collective-permute-done.6.rest_8_), channel_id=1, source_target_pairs={{0,1},{1,0},{2,3},{3,2},{4,5},{5,4},{6,7},{7,6},{8,9},{9,8},{10,11... | collective-permute-start | bytes 663560 | tf_op jit(solution)/shard_map/ppermute | solution.py:224
  56.9 2.1 %collective-permute-start.15 = (bf16[432,256]{1,0:T(8,128)(2,1)}, bf16[432,256]{1,0:T(8,128)(2,1)}, u32[]{:S(2)}, u32[]{:S(2)}) collective-permute-start(bf16[432,256]{1,0:T(8,128)(2,1)} %collective-permute-done.7.rest_9_), channel_id=1, source_target_pairs={{0,1},{1,0},{2,3},{3,2},{4,5},{5,4},{6,7},{7,6},{8,9},{9,8},{10,11... | collective-permute-start | bytes 663560 | tf_op jit(solution)/shard_map/ppermute | solution.py:224
  57.4 1.6 %copy-start = (bf16[32,64,256]{2,1,0:T(8,128)(2,1)}, bf16[32,64,256]{2,1,0:T(8,128)(2,1)S(1)}, u32[]{:S(2)}) copy-start(bf16[32,64,256]{2,1,0:T(8,128)(2,1)S(1)} %all-to-all-done.wire) | copy-start | bytes 3145732
  57.5 1.6 %copy-start.9 = (bf16[864,256]{1,0:T(8,128)(2,1)}, bf16[864,256]{1,0:T(8,128)(2,1)S(1)}, u32[]{:S(2)}) copy-start(bf16[864,256]{1,0:T(8,128)(2,1)S(1)} %collective-permute-done.12.rest_14_) | copy-start | bytes 1327108
  57.5 1.6 %copy-start.10 = (bf16[864,256]{1,0:T(8,128)(2,1)}, bf16[864,256]{1,0:T(8,128)(2,1)S(1)}, u32[]{:S(2)}) copy-start(bf16[864,256]{1,0:T(8,128)(2,1)S(1)} %collective-permute-done.13.rest_15_) | copy-start | bytes 1327108

commit v2 on v1

v2 whole, which is shorter than its diff:
```python
import functools

import jax
import jax.numpy as jnp
from jax import lax
from jax.experimental import pallas as pl
from jax.experimental.pallas import tpu as pltpu
from jax.sharding import Mesh
from jax.sharding import PartitionSpec as P

C = 256
TAPS = 27
ROWS = TAPS * 32
HALF = ROWS // 2
PIECES = 18
PART = 48
VMEM = pl.BlockSpec(memory_space=pltpu.VMEM)
ANY = pl.BlockSpec(memory_space=pl.ANY)


def one_hot(source):
    row = lax.broadcasted_iota(jnp.int32, (C, C), 0)
    column = lax.broadcasted_iota(jnp.int32, (C, C), 1)
    return jnp.where(column == source(row), 1.0, 0.0).astype(jnp.bfloat16)


def select(matrix, rows):
    return jnp.dot(matrix, rows, preferred_element_type=jnp.float32).astype(jnp.bfloat16)


def brick_row(r):
    py, pzh, pzl, zq, yq = r >> 6, (r >> 5) & 1, (r >> 4) & 1, (r >> 2) & 3, r & 3
    return (4 * yq + py) * 16 + 4 * zq + 2 * pzh + pzl


def brick_row_inverse(r):
    by, bz = r >> 4, r & 15
    return ((by & 3) << 6) + ((bz & 3) << 4) + ((bz >> 2) << 2) + (by >> 2)


def wire_row(r, shift):
    pzl, zq, xh, y = r >> 7, (r >> 5) & 3, (r >> 4) & 1, (r & 15) + shift
    found = ((y >> 2) << 6) + (xh << 5) + (pzl << 4) + (zq << 2) + (y & 3)
    return jnp.where((y >= 0) & (y < 16), found, -1)


def wire_row_inverse(r):
    j, xh, pzl, zq, yq = r >> 6, (r >> 5) & 1, (r >> 4) & 1, (r >> 2) & 3, r & 3
    return (pzl << 7) + (zq << 5) + (xh << 4) + (j << 2) + yq


def moved_row(r, shift):
    y = (r & 15) + shift
    return jnp.where((y >= 0) & (y < 16), r + shift, -1)


def in_parts(source, target, sem, parts):
    size = source.shape[0] // parts
    for n in range(parts):
        part = pl.ds(n * size, size)
        pltpu.make_async_copy(source.at[part], target.at[part], sem).start()
    return pltpu.make_async_copy(source, target, sem)


def pack_kernel(brick, wire, held, packed, sem):
    loads = {x: in_parts(brick.at[x], held.at[x], sem.at[0, x], 4) for x in (0, 4, 1, 5, 2, 6, 3, 7)}
    order = one_hot(brick_row)
    stores = []
    for half in range(2):
        for x in (2 * half, 2 * half + 4, 2 * half + 1, 2 * half + 5):
            loads[x].wait()
        for px in (2 * half, 2 * half + 1):
            for xh in range(2):
                rows = select(order, held[px + 4 * xh])
                packed[px * 8 : px * 8 + 8, xh * 32 : xh * 32 + 32, :] = rows.reshape(8, 32, C)
        block = pl.ds(half * 16, 16)
        stores.append(in_parts(packed.at[block], wire.at[block], sem.at[1, half], 16))
    for store in stores:
        store.wait()


def unpack_kernel(wire, brick, placed, sem):
    order = one_hot(brick_row_inverse)
    stores = []
    for half in range(2):
        places = [(px, xh) for px in (2 * half, 2 * half + 1) for xh in range(2)]
        for px, xh in places:
            rows = wire[px * 8 : px * 8 + 8, xh * 32 : xh * 32 + 32, :].reshape(C, C)
            placed[px + 4 * xh] = select(order, rows)
        for px, xh in places:
            x = px + 4 * xh
            stores.append(in_parts(placed.at[x], brick.at[x], sem.at[x], 4))
    for store in stores:
        store.wait()


def start_weights(own, moved, swapped, held, sem):
    k, core = lax.axis_index("dp"), lax.axis_index("core")

    def lay(pieces, n):
        targets = [(k, 0)]
        for step in range(1, 4):
            for owner in (k - step + 8, k + step):
                targets.append((lax.rem(owner, 8), 0))
        targets += [(lax.rem(k + 4, 8), 0), (lax.rem(k + 4, 8), HALF)]
        for m, (piece, (slot, base)) in enumerate(zip((own[n], *pieces), targets)):
            for first in range(0, piece.shape[0], PART):
                source = piece.at[pl.ds(first, PART)]
                target = held.at[n, slot, pl.ds(base + first, PART)]
                pltpu.make_async_copy(source, target, sem.at[n, m]).start()

    @pl.when(core == 0)
    def _():
        lay(moved, 0)
        lay(swapped, 1)

    @pl.when(core != 0)
    def _():
        lay(swapped, 0)
        lay(moved, 1)


def arrivals(part, own, moved, held, sem):
    return [
        pltpu.make_async_copy(piece, held.at[part, 0, pl.ds(0, piece.shape[0])], sem.at[part, n])
        for n, piece in enumerate((own[part], *moved))
    ]


def taps_of(shifted, held, step, tz_from_zi):
    left, right = [], []
    for tz, zi in tz_from_zi:
        for tx in range(3):
            for ty in range(3):
                slab = shifted[ty, :, zi, tx * step * 16 : tx * step * 16 + 256, :]
                left.append(slab.reshape(2 * 256, C))
                tap = (tx * 3 + ty) * 3 + tz
                right.append(held[:, tap * 32 : tap * 32 + 32, :].reshape(C, C))
    return jnp.dot(
        jnp.concatenate(left, axis=1),
        jnp.concatenate(right, axis=0),
        preferred_element_type=jnp.float32,
    )


def block_kernel(wire, fine_bias, coarse_bias, *rest):
    pieces = rest[:PIECES]
    out, received, near, far, held, context, packed, sem, weight_sem = rest[PIECES:]
    load = in_parts(wire, received, sem.at[0], 32)
    moved, swapped = pieces[2:10], pieces[10:]
    own = pieces[:2]
    start_weights(own, moved, swapped, held, weight_sem)
    zero = jnp.zeros((3, 2, 4, 32, C), jnp.bfloat16)
    near[:, :, :, 0:16, :] = zero[:, :, :, :16]
    near[:, :, :, 272:288, :] = zero[:, :, :, :16]
    far[:, :, :, 0:32, :] = zero
    far[:, :, :, 288:320, :] = zero
    load.wait()
    for ty in range(3):
        order = one_hot(functools.partial(wire_row, shift=ty - 1))
        for i in range(8):
            rows = select(order, received[4 * i : 4 * i + 4].reshape(C, C))
            near[ty, :, :, 16 + 32 * i : 48 + 32 * i, :] = rows.reshape(2, 4, 32, C)
    for arrival in arrivals(0, own, moved, held, weight_sem):
        arrival.wait()
    for zo in range(4):
        pairs = [(tz, zo + tz - 1) for tz in range(3) if 0 <= zo + tz - 1 < 4]
        total = taps_of(near, held.at[0], 1, pairs)
        here = near[1, :, zo, 16:272, :].reshape(512, C).astype(jnp.float32)
        middle = (here + jax.nn.gelu(total + fine_bias[...])).astype(jnp.bfloat16)
        far[1, :, zo, 32:288, :] = middle.reshape(2, 256, C)
    for arrival in arrivals(1, own, moved, held, weight_sem):
        arrival.wait()
    for ty in (0, 2):
        order = one_hot(functools.partial(moved_row, shift=2 * (ty - 1)))
        for pzl in range(2):
            for z in range(4):
                far[ty, pzl, z, 32:288, :] = select(order, far[1, pzl, z, 32:288, :])
    for zo in range(4):
        pairs = [(tz, zo + 2 * (tz - 1)) for tz in range(3) if 0 <= zo + 2 * (tz - 1) < 4]
        total = taps_of(far, held.at[1], 2, pairs)
        here = far[1, :, zo, 32:288, :].reshape(512, C).astype(jnp.float32)
        result = (here + jax.nn.gelu(total + coarse_bias[...])).astype(jnp.bfloat16)
        context[:, zo] = result.reshape(2, 256, C)
    order = one_hot(wire_row_inverse)
    stores = []
    for half in range(2):
        for i in range(4 * half, 4 * half + 4):
            rows = select(order, context[:, :, 32 * i : 32 * i + 32, :].reshape(C, C))
            packed[4 * i : 4 * i + 4] = rows.reshape(4, 64, C)
        block = pl.ds(16 * half, 16)
        stores.append(in_parts(packed.at[block], out.at[block], sem.at[1 + half], 16))
    for store in stores:
        store.wait()


def shift(value, by):
    return lax.ppermute(value, "dp", [(k, (k + by) % 8) for k in range(8)])


def swap(value):
    return lax.ppermute(value, "core", [(0, 1), (1, 0)])


def gather_filters(shards):
    own = [shard.reshape(ROWS, C) for shard in shards]
    message = jnp.where(lax.axis_index("core") == 0, *own)
    forward = backward = message
    moved, swapped = [], []
    for step in range(1, 5):
        if step == 4:
            forward, backward = forward[:HALF], backward[HALF:]
        forward = shift(forward, 1)
        backward = shift(backward, -1)
        swapped.append(swap(forward))
        swapped.append(swap(backward))
        moved += [forward, backward]
    return (*own, *moved, *swapped)


def on_device(volume, fine_filter, coarse_filter, fine_bias, coarse_bias):
    brick = volume.reshape(8, 256, C)
    wire_shape = jax.ShapeDtypeStruct((32, 64, C), jnp.bfloat16)

    pieces = gather_filters((fine_filter, coarse_filter))
    outgoing = pl.pallas_call(
        pack_kernel,
        out_shape=wire_shape,
        in_specs=[ANY],
        out_specs=ANY,
        scratch_shapes=[
            pltpu.VMEM((8, 256, C), jnp.bfloat16),
            pltpu.VMEM((32, 64, C), jnp.bfloat16),
            pltpu.SemaphoreType.DMA((2, 8)),
        ],
        name="pack",
    )(brick)
    received = lax.all_to_all(outgoing, ("x", "y", "core"), 0, 0, tiled=True)
    outgoing = pl.pallas_call(
        block_kernel,
        out_shape=wire_shape,
        in_specs=[ANY, VMEM, VMEM] + [ANY] * PIECES,
        out_specs=ANY,
        scratch_shapes=[
            pltpu.VMEM((32, 64, C), jnp.bfloat16),
            pltpu.VMEM((3, 2, 4, 288, C), jnp.bfloat16),
            pltpu.VMEM((3, 2, 4, 320, C), jnp.bfloat16),
            pltpu.VMEM((2, 8, ROWS, C), jnp.bfloat16),
            pltpu.VMEM((2, 4, 256, C), jnp.bfloat16),
            pltpu.VMEM((32, 64, C), jnp.bfloat16),
            pltpu.SemaphoreType.DMA((16,)),
            pltpu.SemaphoreType.DMA((2, 9)),
        ],
        name="block",
    )(received, fine_bias.reshape(1, C), coarse_bias.reshape(1, C), *pieces)
    received = lax.all_to_all(outgoing, ("x", "y", "core"), 0, 0, tiled=True)
    brick = pl.pallas_call(
        unpack_kernel,
        out_shape=jax.ShapeDtypeStruct((8, 256, C), jnp.bfloat16),
        in_specs=[VMEM],
        out_specs=ANY,
        scratch_shapes=[pltpu.VMEM((8, 256, C), jnp.bfloat16), pltpu.SemaphoreType.DMA((8,))],
        compiler_params=pltpu.CompilerParams(vmem_limit_bytes=6 << 20),
        name="unpack",
    )(received)
    return brick.reshape(volume.shape)


def solution(mesh):
    grid = Mesh(mesh.devices.reshape(8, 4, 4, 2), ("dp", "x", "y", "core"))
    space = ("x", "y", "core")
    return jax.shard_map(
        on_device,
        mesh=grid,
        in_specs=(
            P("dp", space, None, None, None, None),
            P(None, None, None, "dp", None),
            P(None, None, None, "dp", None),
            P(),
            P(),
        ),
        out_specs=P("dp", space, None, None, None, None),
        check_vma=False,
    )
```

time: 104 us -> 100 us (0.962)
  Pallas kernels: 25.1 us -> 21.1 us
    pallas_call x2 -> x1, Pallas kernels: 19.9 us -> 17.3 us  [on_device(): pl.pallas_call(block_kernel, out_shape=wire_shape, in_specs=[ANY, VMEM, V...]
    pallas_call x1, Pallas kernels: 2.56 us -> 1.32 us  [on_device(): pl.pallas_call(unpack_kernel, out_shape=jax.ShapeDtypeStruct((8, 256, C),...]
    select_n x0 -> x1, other arithmetic: none -> 1.19 us  [gather_filters(): message = jnp.where(lax.axis_index('core') == 0, *own)]
where the time goes in v2:
time: 100 us; the launch traced here: 99.6 us
  starting transfers between devices  27.8 us (28%)
  waiting for transfers between devices  24.9 us (25%)
  blocking collectives  24.1 us (24%)
  Pallas kernels  21.1 us (21%)
  other arithmetic  1.19 us (1%)
    all_to_all x1, blocking collectives, on_device(): received = lax.all_to_all(outgoing, ('x', 'y', 'core'), 0, 0, tiled=True)  24.1 us
    ppermute x8, waiting for transfers between devices, shift(): return lax.ppermute(value, 'dp', [(k, (k + by) % 8) for k in range(8)])  23.4 us
    pallas_call x1, Pallas kernels, on_device(): pl.pallas_call(block_kernel, out_shape=wire_shape, in_specs=[ANY, VMEM, V...  17.3 us
    ppermute x8, starting transfers between devices, shift(): return lax.ppermute(value, 'dp', [(k, (k + by) % 8) for k in range(8)])  14.6 us
    all_to_all x1, starting transfers between devices, on_device(): received = lax.all_to_all(outgoing, ('x', 'y', 'core'), 0, 0, tiled=True)  8.91 us
    ppermute x8, starting transfers between devices, swap(): return lax.ppermute(value, 'core', [(0, 1), (1, 0)])  4.26 us
    pallas_call x1, Pallas kernels, on_device(): pl.pallas_call(pack_kernel, out_shape=wire_shape, in_specs=[ANY], out_spe...  2.53 us
  transfers between devices with their start and end apart: 17, of which 5 were waited for; matrix products, arithmetic and copies ran while one was open for 0% of the time, Pallas kernels for 3%

profile of v2, /device:TPU:1, one launch (start us, length us, event | category | flops | bytes accessed | tf_op | source)
XLA Modules:
  0.0 99.6 jit_solution(16017026212724976540)
XLA Ops:
  0.0 1.2 %broadcast_select_fusion = bf16[864,256]{1,0:T(8,128)(2,1)S(1)} fusion(pred[]{:T(512)S(6)} %eq.3, bf16[3,3,3,32,256]{4,3,2,1,0:T(8,128)(2,1)} %param.7, bf16[3,3,3,32,256]{4,3,2,1,0:T(8,128)(2,1)} %param.6), kind=kLoop, calls=%fused_computation | loop fusion | flops 221184 | bytes 1327105 | tf_op jit(solution)/shard_map/jit(_where)/select_n | solution.py:207
  1.2 2.5 %collective-permute-start = (bf16[864,256]{1,0:T(8,128)(2,1)S(1)}, bf16[864,256]{1,0:T(8,128)(2,1)S(1)}, u32[]{:S(2)}, u32[]{:S(2)}) collective-permute-start(bf16[864,256]{1,0:T(8,128)(2,1)S(1)} %broadcast_select_fusion), channel_id=1, source_target_pairs={{0,32},{32,64},{64,96},{96,128},{128,160},{160,192},{192,224},{224... | collective-permute-start | bytes 1327112 | tf_op jit(solution)/shard_map/ppermute | solution.py:198
  3.7 4.0 %collective-permute-start.1 = (bf16[864,256]{1,0:T(8,128)(2,1)S(1)}, bf16[864,256]{1,0:T(8,128)(2,1)S(1)}, u32[]{:S(2)}, u32[]{:S(2)}) collective-permute-start(bf16[864,256]{1,0:T(8,128)(2,1)S(1)} %broadcast_select_fusion), channel_id=1, source_target_pairs={{0,224},{32,0},{64,32},{96,64},{128,96},{160,128},{192,160},{224,1... | collective-permute-start | bytes 1327112 | tf_op jit(solution)/shard_map/ppermute | solution.py:198
  7.8 9.8 %collective-permute-done.rest_2_ = bf16[864,256]{1,0:T(8,128)(2,1)S(1)} collective-permute-done((bf16[864,256]{1,0:T(8,128)(2,1)S(1)}, bf16[864,256]{1,0:T(8,128)(2,1)S(1)}, u32[]{:S(2)}, u32[]{:S(2)}) %collective-permute-start) | collective-permute-done | bytes 442400 | tf_op jit(solution)/shard_map/ppermute | solution.py:198
  17.5 0.0 copy-start.3
  17.5 0.0 collective-permute-start.2
  17.5 0.0 collective-permute-done.1.rest_3_
  17.6 0.0 copy-start.4
  17.6 2.7 %collective-permute-start.3 = (bf16[864,256]{1,0:T(8,128)(2,1)S(1)}, bf16[864,256]{1,0:T(8,128)(2,1)}, u32[]{:S(2)}, u32[]{:S(2)}) collective-permute-start(bf16[864,256]{1,0:T(8,128)(2,1)S(1)} %collective-permute-done.1.rest_3_), channel_id=1, source_target_pairs={{0,224},{32,0},{64,32},{96,64},{128,96},{160,128},{192,160},{224,1... | collective-permute-start | bytes 1327112 | tf_op jit(solution)/shard_map/ppermute | solution.py:198
  20.2 2.5 %pack.1 = bf16[32,64,256]{2,1,0:T(8,128)(2,1)} custom-call(bf16[8,256,256]{2,1,0:T(8,128)(2,1)} %bitcast.10), custom_call_target="tpu_custom_call" | custom-call | tf_op jit(solution)/shard_map/pack/pallas_call | solution.py:226
  22.8 8.9 %all-to-all-start = ((bf16[32,64,256]{2,1,0:T(8,128)(2,1)}), bf16[32,64,256]{2,1,0:T(8,128)(2,1)S(1)}, u32[]{:S(2)}, u32[]{:S(2)}) async-start(bf16[32,64,256]{2,1,0:T(8,128)(2,1)} %pack.1), calls=%async_computation | async-start | bytes 2097152 | tf_op jit(solution)/shard_map/all_to_all | solution.py:238
  31.7 0.0 collective-permute-done.2.rest_4_
  31.7 0.0 copy-start.5
  31.7 0.1 collective-permute-start.4
  31.8 0.0 collective-permute-done.3.rest_5_
  31.8 2.7 %collective-permute-start.5 = (bf16[864,256]{1,0:T(8,128)(2,1)}, bf16[864,256]{1,0:T(8,128)(2,1)S(1)}, u32[]{:S(2)}, u32[]{:S(2)}) collective-permute-start(bf16[864,256]{1,0:T(8,128)(2,1)} %collective-permute-done.3.rest_5_), channel_id=1, source_target_pairs={{0,224},{32,0},{64,32},{96,64},{128,96},{160,128},{192,160},{224,1... | collective-permute-start | bytes 1327112 | tf_op jit(solution)/shard_map/ppermute | solution.py:198
  34.5 0.0 copy-done.3
  34.5 0.8 collective-permute-start.8
  35.3 0.0 copy-done.4
  35.3 0.1 collective-permute-start.9
  35.4 0.4 collective-permute-start.10
  35.8 8.7 %collective-permute-done.4.rest_6_ = bf16[864,256]{1,0:T(8,128)(2,1)S(1)} collective-permute-done((bf16[864,256]{1,0:T(8,128)(2,1)S(1)}, bf16[864,256]{1,0:T(8,128)(2,1)S(1)}, u32[]{:S(2)}, u32[]{:S(2)}) %collective-permute-start.4) | collective-permute-done | bytes 442400 | tf_op jit(solution)/shard_map/ppermute | solution.py:198
  44.5 0.0 copy-start.1
  44.5 1.1 %collective-permute-start.11 = (bf16[864,256]{1,0:T(8,128)(2,1)}, bf16[864,256]{1,0:T(8,128)(2,1)}, u32[]{:S(2)}, u32[]{:S(2)}) collective-permute-start(bf16[864,256]{1,0:T(8,128)(2,1)} %collective-permute-done.3.rest_5_), channel_id=1, source_target_pairs={{0,1},{1,0},{2,3},{3,2},{4,5},{5,4},{6,7},{7,6},{8,9},{9,8},{10,11... | collective-permute-start | bytes 1327112 | tf_op jit(solution)/shard_map/ppermute | solution.py:202
  45.6 0.0 collective-permute-done.5.rest_7_
  45.6 0.0 copy-start.2
  45.6 0.1 collective-permute-start.6
  45.7 0.0 collective-permute-done.8.rest_10_
  45.7 0.0 copy-done.1
  45.7 0.0 copy-start.6
  45.8 0.6 collective-permute-start.12
  46.3 0.0 collective-permute-done.9.rest_11_
  46.3 0.0 copy-start.7
  46.3 0.1 collective-permute-start.13
  46.4 0.0 collective-permute-done.10.rest_12_
  46.4 0.0 copy-start.8
  46.4 2.6 %collective-permute-start.7 = (bf16[432,256]{1,0:T(8,128)(2,1)S(1)}, bf16[432,256]{1,0:T(8,128)(2,1)}, u32[]{:S(2)}, u32[]{:S(2)}) collective-permute-start(bf16[432,256]{1,0:T(8,128)(2,1)S(1)} %slice.9), channel_id=1, source_target_pairs={{0,224},{32,0},{64,32},{96,64},{128,96},{160,128},{192,160},{224,1... | collective-permute-start | bytes 663560 | tf_op jit(solution)/shard_map/ppermute | solution.py:198
  49.0 4.9 %collective-permute-done.6.rest_8_ = bf16[432,256]{1,0:T(8,128)(2,1)S(1)} collective-permute-done((bf16[432,256]{1,0:T(8,128)(2,1)S(1)}, bf16[432,256]{1,0:T(8,128)(2,1)S(1)}, u32[]{:S(2)}, u32[]{:S(2)}) %collective-permute-start.6) | collective-permute-done | bytes 221216 | tf_op jit(solution)/shard_map/ppermute | solution.py:198
  53.9 0.0 copy-start.11
  53.9 0.9 collective-permute-start.14
  54.7 0.0 collective-permute-done.7.rest_9_
  54.8 0.0 copy-done.6
  54.8 0.0 copy-done.7
  54.8 0.0 copy-done.8
  54.8 0.3 collective-permute-start.15
  55.1 0.0 all-to-all-done.wire
  55.1 0.0 copy-start
  55.1 0.0 collective-permute-done.11.rest_13_
  55.1 0.0 collective-permute-done.12.rest_14_
  55.1 0.0 copy-start.9
  55.1 0.0 collective-permute-done.13.rest_15_
  55.1 0.0 copy-start.10
  55.1 0.8 collective-permute-done.14.rest_16_
  56.0 0.7 collective-permute-done.15.rest_17_
  56.7 0.0 copy-done.5
  56.7 0.0 copy-done.2
  56.7 0.0 copy-done.11
  56.7 0.0 copy-done
  56.7 0.0 copy-done.9
  56.7 0.0 copy-done.10
  56.7 17.3 %block.1 = bf16[32,64,256]{2,1,0:T(8,128)(2,1)} custom-call(bf16[32,64,256]{2,1,0:T(8,128)(2,1)} %copy-done, f32[1,256]{1,0:T(1,128)} %bitcast.11, f32[1,256]{1,0:T(1,128)} %bitcast.12, bf16[864,256]{1,0:T(8,128)(2,1)} %bitcast.8, bf16[864,256]{1,0:T(8,128)(2,1)} %bitcast.9, bf16[864,256]{1,0:T(8,128)(2,1)} %copy-done.3, bf16[864,256]{1,0:T(8,128)(2,1)} %copy-done.4, ...), custom_call_target="tpu_custom_call" | custom-call | tf_op jit(solution)/shard_map/block/pallas_call | solution.py:239
  74.0 24.1 %all_to_all.10.wire = bf16[32,64,256]{2,1,0:T(8,128)(2,1)S(1)} all-to-all(bf16[32,64,256]{2,1,0:T(8,128)(2,1)} %block.1), channel_id=1, replica_groups=mesh['dp'=8,'x'=4,'y'=4,'core'=2] {'x','y','core'}, dimensions={0} | all-to-all | bytes 2097152 | tf_op jit(solution)/shard_map/all_to_all | solution.py:256
  98.1 1.3 %unpack.1 = bf16[8,256,256]{2,1,0:T(8,128)(2,1)} custom-call(bf16[32,64,256]{2,1,0:T(8,128)(2,1)S(1)} %all_to_all.10.wire), custom_call_target="tpu_custom_call" | custom-call | tf_op jit(solution)/shard_map/unpack/pallas_call | solution.py:257
  (2 shorter events, 0.0 us)
Async XLA Ops:
  1.2 16.3 %collective-permute-start = (bf16[864,256]{1,0:T(8,128)(2,1)S(1)}, bf16[864,256]{1,0:T(8,128)(2,1)S(1)}, u32[]{:S(2)}, u32[]{:S(2)}) collective-permute-start(bf16[864,256]{1,0:T(8,128)(2,1)S(1)} %broadcast_select_fusion), channel_id=1, source_target_pairs={{0,32},{32,64},{64,96},{96,128},{128,160},{160,192},{192,224},{224... | collective-permute-start | bytes 1327112 | tf_op jit(solution)/shard_map/ppermute | solution.py:198
  3.7 13.8 %collective-permute-start.1 = (bf16[864,256]{1,0:T(8,128)(2,1)S(1)}, bf16[864,256]{1,0:T(8,128)(2,1)S(1)}, u32[]{:S(2)}, u32[]{:S(2)}) collective-permute-start(bf16[864,256]{1,0:T(8,128)(2,1)S(1)} %broadcast_select_fusion), channel_id=1, source_target_pairs={{0,224},{32,0},{64,32},{96,64},{128,96},{160,128},{192,160},{224,1... | collective-permute-start | bytes 1327112 | tf_op jit(solution)/shard_map/ppermute | solution.py:198
  17.5 16.9 %copy-start.3 = (bf16[864,256]{1,0:T(8,128)(2,1)}, bf16[864,256]{1,0:T(8,128)(2,1)S(1)}, u32[]{:S(2)}) copy-start(bf16[864,256]{1,0:T(8,128)(2,1)S(1)} %collective-permute-done.rest_2_) | copy-start | bytes 1327108
  17.5 14.1 %collective-permute-start.2 = (bf16[864,256]{1,0:T(8,128)(2,1)S(1)}, bf16[864,256]{1,0:T(8,128)(2,1)S(1)}, u32[]{:S(2)}, u32[]{:S(2)}) collective-permute-start(bf16[864,256]{1,0:T(8,128)(2,1)S(1)} %collective-permute-done.rest_2_), channel_id=1, source_target_pairs={{0,32},{32,64},{64,96},{96,128},{128,160},{160,192},{192,224},{224... | collective-permute-start | bytes 1327112 | tf_op jit(solution)/shard_map/ppermute | solution.py:198
  17.6 17.7 %copy-start.4 = (bf16[864,256]{1,0:T(8,128)(2,1)}, bf16[864,256]{1,0:T(8,128)(2,1)S(1)}, u32[]{:S(2)}) copy-start(bf16[864,256]{1,0:T(8,128)(2,1)S(1)} %collective-permute-done.1.rest_3_) | copy-start | bytes 1327108
  17.6 14.2 %collective-permute-start.3 = (bf16[864,256]{1,0:T(8,128)(2,1)S(1)}, bf16[864,256]{1,0:T(8,128)(2,1)}, u32[]{:S(2)}, u32[]{:S(2)}) collective-permute-start(bf16[864,256]{1,0:T(8,128)(2,1)S(1)} %collective-permute-done.1.rest_3_), channel_id=1, source_target_pairs={{0,224},{32,0},{64,32},{96,64},{128,96},{160,128},{192,160},{224,1... | collective-permute-start | bytes 1327112 | tf_op jit(solution)/shard_map/ppermute | solution.py:198
  22.8 32.3 %all-to-all-start = ((bf16[32,64,256]{2,1,0:T(8,128)(2,1)}), bf16[32,64,256]{2,1,0:T(8,128)(2,1)S(1)}, u32[]{:S(2)}, u32[]{:S(2)}) async-start(bf16[32,64,256]{2,1,0:T(8,128)(2,1)} %pack.1), calls=%async_computation | async-start | bytes 2097152 | tf_op jit(solution)/shard_map/all_to_all | solution.py:238
  31.7 25.0 %copy-start.5 = (bf16[864,256]{1,0:T(8,128)(2,1)}, bf16[864,256]{1,0:T(8,128)(2,1)S(1)}, u32[]{:S(2)}) copy-start(bf16[864,256]{1,0:T(8,128)(2,1)S(1)} %collective-permute-done.2.rest_4_) | copy-start | bytes 1327108
  31.7 12.8 %collective-permute-start.4 = (bf16[864,256]{1,0:T(8,128)(2,1)S(1)}, bf16[864,256]{1,0:T(8,128)(2,1)S(1)}, u32[]{:S(2)}, u32[]{:S(2)}) collective-permute-start(bf16[864,256]{1,0:T(8,128)(2,1)S(1)} %collective-permute-done.2.rest_4_), channel_id=1, source_target_pairs={{0,32},{32,64},{64,96},{96,128},{128,160},{160,192},{192,224},{224... | collective-permute-start | bytes 1327112 | tf_op jit(solution)/shard_map/ppermute | solution.py:198
  31.8 13.8 %collective-permute-start.5 = (bf16[864,256]{1,0:T(8,128)(2,1)}, bf16[864,256]{1,0:T(8,128)(2,1)S(1)}, u32[]{:S(2)}, u32[]{:S(2)}) collective-permute-start(bf16[864,256]{1,0:T(8,128)(2,1)} %collective-permute-done.3.rest_5_), channel_id=1, source_target_pairs={{0,224},{32,0},{64,32},{96,64},{128,96},{160,128},{192,160},{224,1... | collective-permute-start | bytes 1327112 | tf_op jit(solution)/shard_map/ppermute | solution.py:198
  34.5 11.3 %collective-permute-start.8 = (bf16[864,256]{1,0:T(8,128)(2,1)S(1)}, bf16[864,256]{1,0:T(8,128)(2,1)S(1)}, u32[]{:S(2)}, u32[]{:S(2)}) collective-permute-start(bf16[864,256]{1,0:T(8,128)(2,1)S(1)} %collective-permute-done.rest_2_), channel_id=1, source_target_pairs={{0,1},{1,0},{2,3},{3,2},{4,5},{5,4},{6,7},{7,6},{8,9},{9,8},{10,11... | collective-permute-start | bytes 1327112 | tf_op jit(solution)/shard_map/ppermute | solution.py:202
  35.3 11.1 %collective-permute-start.9 = (bf16[864,256]{1,0:T(8,128)(2,1)S(1)}, bf16[864,256]{1,0:T(8,128)(2,1)S(1)}, u32[]{:S(2)}, u32[]{:S(2)}) collective-permute-start(bf16[864,256]{1,0:T(8,128)(2,1)S(1)} %collective-permute-done.1.rest_3_), channel_id=1, source_target_pairs={{0,1},{1,0},{2,3},{3,2},{4,5},{5,4},{6,7},{7,6},{8,9},{9,8},{10,11... | collective-permute-start | bytes 1327112 | tf_op jit(solution)/shard_map/ppermute | solution.py:202
  35.4 11.1 %collective-permute-start.10 = (bf16[864,256]{1,0:T(8,128)(2,1)S(1)}, bf16[864,256]{1,0:T(8,128)(2,1)S(1)}, u32[]{:S(2)}, u32[]{:S(2)}) collective-permute-start(bf16[864,256]{1,0:T(8,128)(2,1)S(1)} %collective-permute-done.2.rest_4_), channel_id=1, source_target_pairs={{0,1},{1,0},{2,3},{3,2},{4,5},{5,4},{6,7},{7,6},{8,9},{9,8},{10,11... | collective-permute-start | bytes 1327112 | tf_op jit(solution)/shard_map/ppermute | solution.py:202
  44.5 1.3 %copy-start.1 = (bf16[864,256]{1,0:T(8,128)(2,1)}, bf16[864,256]{1,0:T(8,128)(2,1)S(1)}, u32[]{:S(2)}) copy-start(bf16[864,256]{1,0:T(8,128)(2,1)S(1)} %collective-permute-done.4.rest_6_) | copy-start | bytes 1327108
  44.5 10.6 %collective-permute-start.11 = (bf16[864,256]{1,0:T(8,128)(2,1)}, bf16[864,256]{1,0:T(8,128)(2,1)}, u32[]{:S(2)}, u32[]{:S(2)}) collective-permute-start(bf16[864,256]{1,0:T(8,128)(2,1)} %collective-permute-done.3.rest_5_), channel_id=1, source_target_pairs={{0,1},{1,0},{2,3},{3,2},{4,5},{5,4},{6,7},{7,6},{8,9},{9,8},{10,11... | collective-permute-start | bytes 1327112 | tf_op jit(solution)/shard_map/ppermute | solution.py:202
  45.6 11.1 %copy-start.2 = (bf16[864,256]{1,0:T(8,128)(2,1)}, bf16[864,256]{1,0:T(8,128)(2,1)S(1)}, u32[]{:S(2)}) copy-start(bf16[864,256]{1,0:T(8,128)(2,1)S(1)} %collective-permute-done.5.rest_7_) | copy-start | bytes 1327108
  45.6 8.3 %collective-permute-start.6 = (bf16[432,256]{1,0:T(8,128)(2,1)S(1)}, bf16[432,256]{1,0:T(8,128)(2,1)S(1)}, u32[]{:S(2)}, u32[]{:S(2)}) collective-permute-start(bf16[432,256]{1,0:T(8,128)(2,1)S(1)} %slice.8), channel_id=1, source_target_pairs={{0,32},{32,64},{64,96},{96,128},{128,160},{160,192},{192,224},{224... | collective-permute-start | bytes 663560 | tf_op jit(solution)/shard_map/ppermute | solution.py:198
  45.7 9.0 %copy-start.6 = (bf16[864,256]{1,0:T(8,128)(2,1)}, bf16[864,256]{1,0:T(8,128)(2,1)S(1)}, u32[]{:S(2)}) copy-start(bf16[864,256]{1,0:T(8,128)(2,1)S(1)} %collective-permute-done.8.rest_10_) | copy-start | bytes 1327108
  45.8 9.4 %collective-permute-start.12 = (bf16[864,256]{1,0:T(8,128)(2,1)S(1)}, bf16[864,256]{1,0:T(8,128)(2,1)S(1)}, u32[]{:S(2)}, u32[]{:S(2)}) collective-permute-start(bf16[864,256]{1,0:T(8,128)(2,1)S(1)} %collective-permute-done.4.rest_6_), channel_id=1, source_target_pairs={{0,1},{1,0},{2,3},{3,2},{4,5},{5,4},{6,7},{7,6},{8,9},{9,8},{10,11... | collective-permute-start | bytes 1327112 | tf_op jit(solution)/shard_map/ppermute | solution.py:202
  46.3 8.4 %copy-start.7 = (bf16[864,256]{1,0:T(8,128)(2,1)}, bf16[864,256]{1,0:T(8,128)(2,1)S(1)}, u32[]{:S(2)}) copy-start(bf16[864,256]{1,0:T(8,128)(2,1)S(1)} %collective-permute-done.9.rest_11_) | copy-start | bytes 1327108
  46.3 8.8 %collective-permute-start.13 = (bf16[864,256]{1,0:T(8,128)(2,1)S(1)}, bf16[864,256]{1,0:T(8,128)(2,1)S(1)}, u32[]{:S(2)}, u32[]{:S(2)}) collective-permute-start(bf16[864,256]{1,0:T(8,128)(2,1)S(1)} %collective-permute-done.5.rest_7_), channel_id=1, source_target_pairs={{0,1},{1,0},{2,3},{3,2},{4,5},{5,4},{6,7},{7,6},{8,9},{9,8},{10,11... | collective-permute-start | bytes 1327112 | tf_op jit(solution)/shard_map/ppermute | solution.py:202
  46.4 8.3 %copy-start.8 = (bf16[864,256]{1,0:T(8,128)(2,1)}, bf16[864,256]{1,0:T(8,128)(2,1)S(1)}, u32[]{:S(2)}) copy-start(bf16[864,256]{1,0:T(8,128)(2,1)S(1)} %collective-permute-done.10.rest_12_) | copy-start | bytes 1327108
  46.4 8.3 %collective-permute-start.7 = (bf16[432,256]{1,0:T(8,128)(2,1)S(1)}, bf16[432,256]{1,0:T(8,128)(2,1)}, u32[]{:S(2)}, u32[]{:S(2)}) collective-permute-start(bf16[432,256]{1,0:T(8,128)(2,1)S(1)} %slice.9), channel_id=1, source_target_pairs={{0,224},{32,0},{64,32},{96,64},{128,96},{160,128},{192,160},{224,1... | collective-permute-start | bytes 663560 | tf_op jit(solution)/shard_map/ppermute | solution.py:198
  53.9 2.8 %copy-start.11 = (bf16[432,256]{1,0:T(8,128)(2,1)}, bf16[432,256]{1,0:T(8,128)(2,1)S(1)}, u32[]{:S(2)}) copy-start(bf16[432,256]{1,0:T(8,128)(2,1)S(1)} %collective-permute-done.6.rest_8_) | copy-start | bytes 663556
  53.9 2.1 %collective-permute-start.14 = (bf16[432,256]{1,0:T(8,128)(2,1)S(1)}, bf16[432,256]{1,0:T(8,128)(2,1)}, u32[]{:S(2)}, u32[]{:S(2)}) collective-permute-start(bf16[432,256]{1,0:T(8,128)(2,1)S(1)} %collective-permute-done.6.rest_8_), channel_id=1, source_target_pairs={{0,1},{1,0},{2,3},{3,2},{4,5},{5,4},{6,7},{7,6},{8,9},{9,8},{10,11... | collective-permute-start | bytes 663560 | tf_op jit(solution)/shard_map/ppermute | solution.py:202
  54.8 1.9 %collective-permute-start.15 = (bf16[432,256]{1,0:T(8,128)(2,1)}, bf16[432,256]{1,0:T(8,128)(2,1)}, u32[]{:S(2)}, u32[]{:S(2)}) collective-permute-start(bf16[432,256]{1,0:T(8,128)(2,1)} %collective-permute-done.7.rest_9_), channel_id=1, source_target_pairs={{0,1},{1,0},{2,3},{3,2},{4,5},{5,4},{6,7},{7,6},{8,9},{9,8},{10,11... | collective-permute-start | bytes 663560 | tf_op jit(solution)/shard_map/ppermute | solution.py:202
  55.1 1.6 %copy-start = (bf16[32,64,256]{2,1,0:T(8,128)(2,1)}, bf16[32,64,256]{2,1,0:T(8,128)(2,1)S(1)}, u32[]{:S(2)}) copy-start(bf16[32,64,256]{2,1,0:T(8,128)(2,1)S(1)} %all-to-all-done.wire) | copy-start | bytes 3145732
  55.1 1.6 %copy-start.9 = (bf16[864,256]{1,0:T(8,128)(2,1)}, bf16[864,256]{1,0:T(8,128)(2,1)S(1)}, u32[]{:S(2)}) copy-start(bf16[864,256]{1,0:T(8,128)(2,1)S(1)} %collective-permute-done.12.rest_14_) | copy-start | bytes 1327108
  55.1 1.6 %copy-start.10 = (bf16[864,256]{1,0:T(8,128)(2,1)}, bf16[864,256]{1,0:T(8,128)(2,1)S(1)}, u32[]{:S(2)}) copy-start(bf16[864,256]{1,0:T(8,128)(2,1)S(1)} %collective-permute-done.13.rest_15_) | copy-start | bytes 1327108
